TPU v7x, 512 devices: a whole 4x4x16 slice. The times are simulated.
512 devices in a mesh: dp: 32 (over z, y_hi), expert: 16 (over y_lo, x, core).
Axes of the slice: x: 4, y: 4 (y_hi: 2, y_lo: 2; y = y_hi * 2 + y_lo), z: 16, core: 2. Of those that a mesh axis runs over, the one named last changes fastest.
Arguments:
- weight: bfloat16 [16, 1024, 4096], P('expert', None, 'dp'), may hold values from -0.1875 to 0.1875
- first_moment: float32 [16, 1024, 4096], P('expert', None, 'dp'), may hold values from -3 to 3
- second_moment: float32 [16, 1024, 4096], P('expert', None, 'dp'), may hold values from 0.01 to 1
- gate_act: bfloat16 [16, 4096, 1024], P('expert', 'dp'), may hold values from -6 to 6
- up_act: bfloat16 [16, 4096, 1024], P('expert', 'dp'), may hold values from -6 to 6
- out_grad: bfloat16 [16, 4096, 4096], P('expert', 'dp'), may hold values from -0.29882812 to 0.29882812
- old_host: int32 [16], replicated, may hold values from 0 to 15, each once
- new_host: int32 [16], replicated, may hold values from 0 to 15, each once
- counts: int32 [32, 16], replicated, may hold values from 1 to 128, as said below
Outputs:
- expert_out: bfloat16 [16, 4096, 4096], P('expert', 'dp')
- new_weight: bfloat16 [16, 1024, 4096], P('expert', None, 'dp')
- new_first: float32 [16, 1024, 4096], P('expert', None, 'dp')
- new_second: float32 [16, 1024, 4096], P('expert', None, 'dp')
Inputs may be any that keep to these rules, and one draw needn't show every extreme that they name: `old_host`: each expert's host index appears once. `new_host`: each expert's host index appears once. `counts`: some expert from some replica fills all 128 slots.
All inputs are finite; a program needn't handle non-finite values.
Results may differ from a plain program's by a relative error of at most 0.0049.
Values may be sent and summed in bfloat16 or wider, within the bound.
No kernel may reach another device: no remote copies, remote signals or barrier semaphores. Data moves between devices by JAX's collectives and lax.ppermute only.
A program may use at most 64 MiB of HBM per device.

v0:
```python
import jax
import jax.numpy as jnp
from jax import lax
from jax.sharding import PartitionSpec as P

beta_one = 0.9
beta_two = 0.999
learning_rate = 0.001
epsilon_value = 1e-08
bias_one = 0.9999734386011124
bias_two = 0.0952078528863


def local(
    weight, first_moment, second_moment, gate_act, up_act, out_grad, old_host, new_host, counts
):
    host_count = lax.axis_size("expert")
    my_host = lax.axis_index("expert")
    my_replica = lax.axis_index("dp")
    expert_ids = jnp.arange(new_host.shape[0], dtype=jnp.int32)
    host_ids = jnp.arange(host_count, dtype=jnp.int32)
    matches = new_host[None, :] == host_ids[:, None]
    source_of = jnp.sum(jnp.where(matches, old_host[None, :], 0), axis=1)
    expert_of = jnp.sum(jnp.where(matches, expert_ids[None, :], 0), axis=1)
    my_expert = expert_of[my_host]
    my_source = source_of[my_host]
    hidden_units = weight.shape[1]
    columns = weight.shape[2]
    block_rows = hidden_units // host_count

    def reorder(received):
        return received.reshape(host_count, block_rows, columns)[source_of].reshape(
            hidden_units, columns
        )

    shards = lax.all_gather(weight, "expert", axis=0, tiled=True)
    picked = jnp.arange(shards.shape[0], dtype=jnp.int32) == my_source
    moved_weight = jnp.sum(jnp.where(picked[:, None, None], shards, jnp.zeros_like(shards)), axis=0)
    spread_first, spread_second = (
        lax.all_to_all(first_moment[0], "expert", split_axis=0, concat_axis=0, tiled=True),
        lax.all_to_all(second_moment[0], "expert", split_axis=0, concat_axis=0, tiled=True),
    )
    moved_first, moved_second = (
        lax.all_to_all(reorder(spread_first), "expert", split_axis=0, concat_axis=0, tiled=True),
        lax.all_to_all(reorder(spread_second), "expert", split_axis=0, concat_axis=0, tiled=True),
    )
    live_rows = counts[:, my_expert]
    slot_ids = jnp.arange(gate_act.shape[1], dtype=jnp.int32)
    filled = slot_ids < live_rows[my_replica]
    activated = jax.nn.silu(gate_act[0].astype(jnp.float32)) * up_act[0].astype(jnp.float32)
    hidden = jnp.where(filled[:, None], activated, jnp.float32(0.0)).astype(jnp.bfloat16)
    grad_columns = lax.all_to_all(out_grad[0], "dp", split_axis=1, concat_axis=0, tiled=True)
    shards = lax.all_gather(hidden, "dp", axis=0, tiled=True)
    grad_sum = jnp.einsum("rf,rc->fc", shards, grad_columns, preferred_element_type=jnp.float32)
    produced = jnp.dot(shards, moved_weight, preferred_element_type=jnp.float32).astype(
        jnp.bfloat16
    )
    output_columns = produced
    grad_sum, output_columns = (grad_sum, output_columns)
    output = lax.all_to_all(output_columns, "dp", split_axis=0, concat_axis=1, tiled=True)
    new_first = beta_one * moved_first + (1.0 - beta_one) * grad_sum
    new_second = beta_two * moved_second + (1.0 - beta_two) * grad_sum * grad_sum
    update = (
        learning_rate * (new_first / bias_one) / (jnp.sqrt(new_second / bias_two) + epsilon_value)
    )
    new_weight = (moved_weight.astype(jnp.float32) - update).astype(jnp.bfloat16)
    return (output[None], new_weight[None], new_first[None], new_second[None])


def solution(mesh):
    return jax.shard_map(
        local,
        mesh=mesh,
        in_specs=(
            P("expert", None, "dp"),
            P("expert", None, "dp"),
            P("expert", None, "dp"),
            P("expert", "dp", None),
            P("expert", "dp", None),
            P("expert", "dp", None),
            P(),
            P(),
            P(),
        ),
        out_specs=(
            P("expert", "dp", None),
            P("expert", None, "dp"),
            P("expert", None, "dp"),
            P("expert", None, "dp"),
        ),
        check_vma=False,
    )
```

profile of v0, /device:TPU:6, one launch (start us, length us, event | category | flops | bytes accessed | tf_op | source)
XLA Modules:
  0.0 364.7 jit_solution(6703636606916573695)
XLA Ops:
  7.2 0.7 all-gather.5.cloned.1.call-update
  7.9 0.8 select_reduce_fusion.1
  11.3 1.3 dynamic_slice.11
  13.2 1.9 fusion.6
  15.2 17.3 %all_to_all.65 = f32[16,64,128]{2,1,0:T(8,128)S(1)} all-to-all(f32[16,64,128]{2,1,0:T(8,128)} %bitcast.38), channel_id=1, replica_groups=mesh['dp'=32,'expert'=16] {'expert'}, dimensions={0} | all-to-all | bytes 1048576 | tf_op jit(solution)/shard_map/all_to_all | solution.py:41
  32.4 6.4 %all-to-all-start.1 = ((f32[16,64,128]{2,1,0:T(8,128)}), f32[16,64,128]{2,1,0:T(8,128)S(1)}, u32[]{:S(2)}, u32[]{:S(2)}) async-start(f32[16,64,128]{2,1,0:T(8,128)} %bitcast.39), calls=%async_computation.1 | async-start | bytes 1048576 | tf_op jit(solution)/shard_map/all_to_all | solution.py:40
  38.8 1.4 gather_fusion.1
  40.2 11.5 %all-to-all-done.1 = f32[16,64,128]{2,1,0:T(8,128)S(1)} async-done(((f32[16,64,128]{2,1,0:T(8,128)}), f32[16,64,128]{2,1,0:T(8,128)S(1)}, u32[]{:S(2)}, u32[]{:S(2)}) %all-to-all-start.1) | async-done | bytes 524320 | tf_op jit(solution)/shard_map/all_to_all | solution.py:40
  51.7 5.5 %all-to-all-start.5 = ((f32[16,64,128]{2,1,0:T(8,128)}), f32[16,64,128]{2,1,0:T(8,128)S(1)}, u32[]{:S(2)}, u32[]{:S(2)}) async-start(f32[16,64,128]{2,1,0:T(8,128)} %gather_fusion.1), calls=%async_computation.5 | async-start | bytes 1048576 | tf_op jit(solution)/shard_map/all_to_all | solution.py:45
  57.1 1.4 gather_fusion
  58.5 7.9 %all-to-all-done.5 = f32[16,64,128]{2,1,0:T(8,128)S(1)} async-done(((f32[16,64,128]{2,1,0:T(8,128)}), f32[16,64,128]{2,1,0:T(8,128)S(1)}, u32[]{:S(2)}, u32[]{:S(2)}) %all-to-all-start.5) | async-done | bytes 524320 | tf_op jit(solution)/shard_map/all_to_all | solution.py:45
  66.4 5.4 %all-to-all-start.2 = ((f32[16,64,128]{2,1,0:T(8,128)}), f32[16,64,128]{2,1,0:T(8,128)S(1)}, u32[]{:S(2)}, u32[]{:S(2)}) async-start(f32[16,64,128]{2,1,0:T(8,128)} %gather_fusion), calls=%async_computation.2 | async-start | bytes 1048576 | tf_op jit(solution)/shard_map/all_to_all | solution.py:44
  71.8 2.3 copy.22
  74.1 5.7 %all-to-all-done.2 = f32[16,64,128]{2,1,0:T(8,128)S(1)} async-done(((f32[16,64,128]{2,1,0:T(8,128)}), f32[16,64,128]{2,1,0:T(8,128)S(1)}, u32[]{:S(2)}, u32[]{:S(2)}) %all-to-all-start.2) | async-done | bytes 524320 | tf_op jit(solution)/shard_map/all_to_all | solution.py:44
  79.8 14.5 %all-to-all-start.3 = ((bf16[128,32,128]{0,2,1:T(8,128)(2,1)}), bf16[128,32,128]{0,2,1:T(8,128)(2,1)S(1)}, u32[]{:S(2)}, u32[]{:S(2)}) async-start(bf16[128,32,128]{0,2,1:T(8,128)(2,1)} %bitcast.12), calls=%async_computation.3 | async-start | bytes 2097152 | tf_op jit(solution)/shard_map/all_to_all | solution.py:52
  95.5 3.1 select_reduce_fusion
  98.6 196.2 %all-gather.3.cloned.1.call-done = bf16[4096,1024]{1,0:T(8,128)(2,1)} async-done(((bf16[128,1024]{1,0:T(8,128)(2,1)}), bf16[4096,1024]{1,0:T(8,128)(2,1)}) %all-gather.3.cloned.1.call-update) | async-done | bytes 8388624 | tf_op jit(solution)/shard_map/all_gather | solution.py:53
  294.8 6.7 %convolution_convert_fusion = bf16[4096,128]{1,0:T(8,128)(2,1)} fusion(bf16[4096,1024]{1,0:T(8,128)(2,1)} %all-gather.3.cloned.1.call-done, bf16[1024,128]{1,0:T(8,128)(2,1)S(1)} %select_reduce_fusion), kind=kOutput, calls=%fused_computation.2 | convolution fusion | flops 1074266112 | bytes 9699328 | tf_op jit(solution)/shard_map/dot_general | solution.py:55
  301.5 7.6 %all-to-all-start = ((bf16[32,128,128]{2,1,0:T(8,128)(2,1)}), bf16[32,128,128]{2,1,0:T(8,128)(2,1)S(1)}, u32[]{:S(2)}, u32[]{:S(2)}) async-start(bf16[32,128,128]{2,1,0:T(8,128)(2,1)} %bitcast.36), calls=%async_computation | async-start | bytes 2097152 | tf_op jit(solution)/shard_map/all_to_all | solution.py:60
  309.1 0.9 broadcast_multiply_fusion
  310.0 0.9 broadcast_multiply_fusion.1
  311.6 7.1 %fusion.7 = (bf16[1,1024,128]{2,1,0:T(8,128)(2,1)}, f32[1024,128]{1,0:T(8,128)}, f32[1024,128]{1,0:T(8,128)}) fusion(bf16[1024,128]{1,0:T(8,128)(2,1)S(1)} %select_reduce_fusion, f32[16,64,128]{2,1,0:T(8,128)} %broadcast_multiply_fusion.1, f32[16,64,128]{2,1,0:T(8,128)} %broadcast_multiply_fusion, bf16[4096,1024]{1,0:T(8,128)(2,1)} %all-gather.3.cloned.1.call-done, ...), kind=kOutput, calls=%fused_computation.18 | convolution fusion | flops 1075314688 | bytes 12058624 | tf_op jit(solution)/shard_map/rf,rc->fc/dot_general | solution.py:54
  318.7 37.2 %all-to-all-done = bf16[32,128,128]{2,1,0:T(8,128)(2,1)S(1)} async-done(((bf16[32,128,128]{2,1,0:T(8,128)(2,1)}), bf16[32,128,128]{2,1,0:T(8,128)(2,1)S(1)}, u32[]{:S(2)}, u32[]{:S(2)}) %all-to-all-start) | async-done | bytes 1048608 | tf_op jit(solution)/shard_map/all_to_all | solution.py:60
  356.6 1.3 broadcast_in_dim.68
  (13 shorter events, 3.9 us)
Async XLA Ops:
  7.2 88.3 %all-gather.5.cloned.1.call-start = ((), (), s32[]{:S(2)}) async-start(), calls=%async_computation.7 | async-start | bytes 4456448 | tf_op jit(solution)/shard_map/all_gather | solution.py:36
  7.9 286.9 %all-gather.3.cloned.1.call-start = ((), (), s32[]{:S(2)}) async-start(), calls=%async_computation.6 | async-start | bytes 8650752 | tf_op jit(solution)/shard_map/all_gather | solution.py:53
  32.4 19.2 %all-to-all-start.1 = ((f32[16,64,128]{2,1,0:T(8,128)}), f32[16,64,128]{2,1,0:T(8,128)S(1)}, u32[]{:S(2)}, u32[]{:S(2)}) async-start(f32[16,64,128]{2,1,0:T(8,128)} %bitcast.39), calls=%async_computation.1 | async-start | bytes 1048576 | tf_op jit(solution)/shard_map/all_to_all | solution.py:40
  51.7 14.7 %all-to-all-start.5 = ((f32[16,64,128]{2,1,0:T(8,128)}), f32[16,64,128]{2,1,0:T(8,128)S(1)}, u32[]{:S(2)}, u32[]{:S(2)}) async-start(f32[16,64,128]{2,1,0:T(8,128)} %gather_fusion.1), calls=%async_computation.5 | async-start | bytes 1048576 | tf_op jit(solution)/shard_map/all_to_all | solution.py:45
  66.4 13.4 %all-to-all-start.2 = ((f32[16,64,128]{2,1,0:T(8,128)}), f32[16,64,128]{2,1,0:T(8,128)S(1)}, u32[]{:S(2)}, u32[]{:S(2)}) async-start(f32[16,64,128]{2,1,0:T(8,128)} %gather_fusion), calls=%async_computation.2 | async-start | bytes 1048576 | tf_op jit(solution)/shard_map/all_to_all | solution.py:44
  79.8 221.7 %all-to-all-start.3 = ((bf16[128,32,128]{0,2,1:T(8,128)(2,1)}), bf16[128,32,128]{0,2,1:T(8,128)(2,1)S(1)}, u32[]{:S(2)}, u32[]{:S(2)}) async-start(bf16[128,32,128]{0,2,1:T(8,128)(2,1)} %bitcast.12), calls=%async_computation.3 | async-start | bytes 2097152 | tf_op jit(solution)/shard_map/all_to_all | solution.py:52
  301.5 54.4 %all-to-all-start = ((bf16[32,128,128]{2,1,0:T(8,128)(2,1)}), bf16[32,128,128]{2,1,0:T(8,128)(2,1)S(1)}, u32[]{:S(2)}, u32[]{:S(2)}) async-start(bf16[32,128,128]{2,1,0:T(8,128)(2,1)} %bitcast.36), calls=%async_computation | async-start | bytes 2097152 | tf_op jit(solution)/shard_map/all_to_all | solution.py:60
Sparse Core Ops, SparseCore 0:
  10.1 57.2 all-gather.4
  71.1 223.6 all-gather.2
where the time goes:
time: 366 us; the launch traced here: 365 us
  waiting for transfers between devices  259 us (71%)
  starting transfers between devices  39.4 us (11%)
  blocking collectives  17.3 us (5%)
  between operations  16.1 us (4%)
  matrix products  13.8 us (4%)
  local copies, waits for them, and re-layouts  10.1 us (3%)
  other arithmetic  8.89 us (2%)
    all_gather x1, waiting for transfers between devices, local(): shards = lax.all_gather(hidden, 'dp', axis=0, tiled=True)  196 us
    all_to_all x1, waiting for transfers between devices, local(): lax.all_to_all(output_columns, 'dp', split_axis=0, concat_axis=1, tiled=T...  37.2 us
    all_to_all x1, blocking collectives, local(): lax.all_to_all(second_moment[0], 'expert', split_axis=0, concat_axis=0, t...  17.3 us
    all_to_all x1, starting transfers between devices, local(): lax.all_to_all(out_grad[0], 'dp', split_axis=1, concat_axis=0, tiled=True)  14.5 us
    all_to_all x1, waiting for transfers between devices, local(): lax.all_to_all(first_moment[0], 'expert', split_axis=0, concat_axis=0, ti...  11.5 us
    all_to_all x1, waiting for transfers between devices, local(): lax.all_to_all(reorder(spread_second), 'expert', split_axis=0, concat_axi...  7.88 us
    all_to_all x1, starting transfers between devices, local(): lax.all_to_all(output_columns, 'dp', split_axis=0, concat_axis=1, tiled=T...  7.59 us
  transfers between devices with their start and end apart: 7, of which 5 were waited for; matrix products, arithmetic and copies ran while one was open for 8% of the time, Pallas kernels for 0%

commit v1 on v0

v1 whole, which is shorter than its diff:
```python
import functools

import jax
import jax.numpy as jnp
from jax import lax
from jax.experimental import pallas as pl
from jax.experimental.pallas import tpu as pltpu
from jax.sharding import Mesh, PartitionSpec as P

beta_one = 0.9
beta_two = 0.999
learning_rate = 0.001
epsilon_value = 1e-08
bias_one = 0.9999734386011124
bias_two = 0.0952078528863

N_FAR = 8
N_Z = 16
TEAM = ("near", "half")
SWAP = [(0, 1), (1, 0)]
UP = [(i, (i + 1) % N_FAR) for i in range(N_FAR)]
DOWN = [(i, (i - 1) % N_FAR) for i in range(N_FAR)]
VMEM = pl.BlockSpec(memory_space=pltpu.VMEM)
SMEM = pl.BlockSpec(memory_space=pltpu.SMEM)
ANY = pl.BlockSpec(memory_space=pl.ANY)
FIRST = [4, 3, -3]
SECOND = [2, -2, 1, -1, 0]


def shape(dims, dtype=jnp.bfloat16):
    return jax.ShapeDtypeStruct(dims, dtype)


def cost(flops, moved):
    return pl.CostEstimate(flops=flops, bytes_accessed=moved, transcendentals=0)


def prepare_kernel(place, new_host, counts, gate, up, cotangent, one, two):
    ring, member, host = place[0], place[1], place[2]
    expert = jnp.int32(0)
    for k in range(new_host.shape[0]):
        expert = jnp.where(new_host[k] == host, k, expert)
    live = counts[ring * 4 + member, expert]
    value = gate[...].astype(jnp.float32)
    activated = value / (1.0 + jnp.exp(-value)) * up[...].astype(jnp.float32)
    slot = lax.broadcasted_iota(jnp.int32, activated.shape, 0)
    hidden = jnp.where(slot < live, activated, 0.0).astype(one.dtype)
    for mate in range(4):
        for k in range(hidden.shape[1] // 128):
            one[mate, len(FIRST) + k] = hidden[:, k * 128 : (k + 1) * 128]
    for group, blocks in ((FIRST, one), (SECOND, two)):
        for i, distance in enumerate(group):
            owner = lax.rem(ring + (distance + N_FAR), N_FAR) * 4
            for mate in range(4):
                start = pl.multiple_of((owner + mate) * 128, 128)
                blocks[mate, i] = cotangent[:, pl.ds(start, 128)]


def prepare(place, new_host, counts, gate, up, cotangent):
    return pl.pallas_call(
        prepare_kernel,
        out_shape=[
            shape((4, len(FIRST) + gate.shape[1] // 128, gate.shape[0], 128)),
            shape((4, len(SECOND), gate.shape[0], 128)),
        ],
        in_specs=[SMEM] * 3 + [VMEM] * 3,
        out_specs=[VMEM] * 2,
        cost_estimate=cost(0, 3 << 20),
        name="prepare",
    )(place, new_host, counts, gate, up, cotangent)


def part_of(blocks, i, rows):
    block = jnp.concatenate([blocks[mate, i] for mate in range(4)], axis=0)
    total = lax.dot_general(
        block, rows[...], (((0,), (0,)), ((), ())), preferred_element_type=jnp.float32
    )
    return total.astype(rows.dtype)


def first_kernel(blocks, after, rows, low, high, *out):
    size = blocks.shape[2]
    for mate in range(4):
        for k in range(blocks.shape[1] - len(FIRST)):
            rows[pl.ds(mate * size, size), pl.ds(k * 128, 128)] = blocks[mate, len(FIRST) + k]
    total = part_of(blocks, 0, rows)
    half = total.shape[0] // 2
    low[...] = total[:half]
    high[...] = total[half:]
    for i, ref in enumerate(out):
        ref[...] = part_of(blocks, i + 1, rows)


def first_parts(blocks, after):
    columns, hidden_units = blocks.shape[3], (blocks.shape[1] - len(FIRST)) * 128
    return pl.pallas_call(
        first_kernel,
        out_shape=[shape((4 * blocks.shape[2], hidden_units))]
        + [shape((columns // 2, hidden_units))] * 2
        + [shape((columns, hidden_units))] * (len(FIRST) - 1),
        in_specs=[VMEM, ANY],
        out_specs=[VMEM] * (len(FIRST) + 2),
        cost_estimate=cost(1 << 28, 3 << 20),
        name="first_parts",
    )(blocks, after)


def second_kernel(blocks, rows, *out):
    for i, ref in enumerate(out):
        ref[...] = part_of(blocks, i, rows)


def second_parts(blocks, rows):
    return pl.pallas_call(
        second_kernel,
        out_shape=[shape((blocks.shape[3], rows.shape[1]))] * len(SECOND),
        in_specs=[VMEM] * 2,
        out_specs=[VMEM] * len(SECOND),
        cost_estimate=cost(1 << 29, 3 << 20),
        name="second_parts",
    )(blocks, rows)


def produce_kernel(mate, place, rows, blocks, out):
    member = place[1]
    if mate:
        member = member + 1 - 2 * lax.rem(member, 2)
    size = out.shape[1]
    mine = rows[pl.ds(pl.multiple_of(member * size, size), size), :]
    for i in range(blocks.shape[0]):
        out[i] = jnp.dot(mine, blocks[i], preferred_element_type=jnp.float32).astype(out.dtype)


def produce(mate, place, rows, blocks):
    count, hidden_units, columns = blocks.shape
    size, step = rows.shape[0] // 4, 4
    return pl.pallas_call(
        functools.partial(produce_kernel, mate),
        out_shape=shape((count, size, columns)),
        grid=(count // step,),
        in_specs=[
            SMEM,
            pl.BlockSpec(rows.shape, lambda i: (0, 0)),
            pl.BlockSpec((step, hidden_units, columns), lambda i: (i, 0, 0)),
        ],
        out_specs=pl.BlockSpec((step, size, columns), lambda i: (i, 0, 0)),
        cost_estimate=cost(count << 25, 5 << 20),
        name="produce",
    )(place, rows, blocks)


def reorder_kernel(old_host, new_host, value, *refs):
    out = refs[-1]
    for k in range(value.shape[0]):
        out[new_host[k]] = value[old_host[k]]


def reorder(value, old_host, new_host, after):
    return pl.pallas_call(
        reorder_kernel,
        out_shape=shape(value.shape, value.dtype),
        in_specs=[SMEM] * 2 + [VMEM] + [ANY] * len(after),
        out_specs=VMEM,
        cost_estimate=cost(0, 2 * value.size * value.dtype.itemsize),
        name="reorder",
    )(old_host, new_host, value, *after)


def relocate(blocks, old_host, new_host, *after):
    spread = lax.all_to_all(blocks, "expert", split_axis=0, concat_axis=0, tiled=True)
    ordered = reorder(spread, old_host, new_host, after)
    return lax.all_to_all(ordered, "expert", split_axis=0, concat_axis=0, tiled=True)


def assemble_kernel(place, near, far, out):
    half = lax.rem(place[1], 2)
    for owner in range(N_Z):
        for side, ref in ((half, near), (1 - half, far)):
            start = pl.multiple_of((2 * owner + side) * 128, 128)
            out[:, pl.ds(start, 128)] = ref[owner]


def assemble(place, near, far):
    return pl.pallas_call(
        assemble_kernel,
        out_shape=shape((near.shape[1], 2 * N_Z * 128)),
        in_specs=[SMEM] + [VMEM] * 2,
        out_specs=VMEM,
        cost_estimate=cost(0, 2 << 20),
        name="assemble",
    )(place, near, far)


def adam_kernel(weight, moments, part, rising, falling, new_weight, new_first, new_second):
    hosts, both, _ = moments.shape
    step = both // 2
    grad = part[...].astype(jnp.float32) + rising[...].astype(jnp.float32)
    grad = (grad + falling[...].astype(jnp.float32)).T
    for d in range(hosts):
        at = pl.ds(d * step, step)
        g = grad[d * step : (d + 1) * step]
        first = beta_one * moments[d, :step] + (1.0 - beta_one) * g
        second = beta_two * moments[d, step:] + (1.0 - beta_two) * g * g
        update = (
            learning_rate * (first / bias_one) / (jnp.sqrt(second / bias_two) + epsilon_value)
        )
        new_first[at] = first
        new_second[at] = second
        new_weight[at] = (weight[at].astype(jnp.float32) - update).astype(new_weight.dtype)


def adam(weight, moments, part, rising, falling):
    return pl.pallas_call(
        adam_kernel,
        out_shape=[
            shape(weight.shape),
            shape(weight.shape, jnp.float32),
            shape(weight.shape, jnp.float32),
        ],
        in_specs=[VMEM] * 5,
        out_specs=[VMEM] * 3,
        cost_estimate=cost(0, 3 << 20),
        name="adam",
    )(weight, moments, part, rising, falling)


def add(left, right):
    return (left.astype(jnp.float32) + right.astype(jnp.float32)).astype(jnp.bfloat16)


def local(
    weight, first_moment, second_moment, gate_act, up_act, out_grad, old_host, new_host, counts
):
    hosts = lax.axis_size("expert")
    ring, member = lax.axis_index("ring"), lax.axis_index(TEAM)
    at = jnp.arange(3, dtype=jnp.int32)
    place = jnp.where(at == 0, ring, jnp.where(at == 1, member, lax.axis_index("expert")))
    hidden_units, columns = weight.shape[1:]
    block_rows = hidden_units // hosts
    half = columns // 2

    one, two = prepare(place, new_host, counts, gate_act[0], up_act[0], out_grad[0])
    one = lax.all_to_all(one, TEAM, split_axis=0, concat_axis=0, tiled=True)
    two = lax.all_to_all(two, TEAM, split_axis=0, concat_axis=0, tiled=True)
    spread = lax.all_to_all(
        weight.reshape(hosts, block_rows, columns), "expert", split_axis=0, concat_axis=0, tiled=True
    )
    ordered = reorder(spread, old_host, new_host, [])
    moved_weight = lax.all_to_all(ordered, "expert", split_axis=0, concat_axis=0, tiled=True)
    moved_weight = moved_weight.reshape(hidden_units, columns)
    rows, low, high, *part = first_parts(one, ordered)
    part = dict(zip(FIRST[1:] + SECOND, [*part, *second_parts(two, rows)]))

    gathered = lax.all_gather(moved_weight, ("ring", "near"), axis=0, tiled=False)
    far = lax.ppermute(produce(True, place, rows, gathered), "half", SWAP)
    output = assemble(place, produce(False, place, rows, gathered), far)

    up_sum, down_sum = low, high
    for step in range(1, N_FAR // 2 + 1):
        up_sum = lax.ppermute(up_sum, "ring", UP)
        down_sum = lax.ppermute(down_sum, "ring", DOWN)
        if step < N_FAR // 2:
            up_part, down_part = part[N_FAR // 2 - step], part[step - N_FAR // 2]
            if step == 1:
                up_sum = jnp.concatenate([add(up_sum, up_part[:half]), up_part[half:]])
                down_sum = jnp.concatenate([down_part[:half], add(down_sum, down_part[half:])])
            else:
                up_sum, down_sum = add(up_sum, up_part), add(down_sum, down_part)
        if step == 1:
            stacked = jnp.concatenate(
                [
                    first_moment.reshape(hosts, block_rows, columns),
                    second_moment.reshape(hosts, block_rows, columns),
                ],
                axis=1,
            )
            stacked, up_sum = lax.optimization_barrier((stacked, up_sum))
            moments = relocate(stacked, old_host, new_host)
        if step == 3:
            up_sum, moments = lax.optimization_barrier((up_sum, moments))
    new_weight, new_first, new_second = adam(moved_weight, moments, part[0], up_sum, down_sum)
    return (output[None], new_weight[None], new_first[None], new_second[None])


def solution(mesh):
    hosts = mesh.shape["expert"]
    grid = Mesh(mesh.devices.reshape(N_FAR, 2, 2, hosts), ("ring", "near", "half", "expert"))
    shards = P("expert", None, ("ring", "near", "half"))
    tokens = P("expert", ("ring", "near", "half"), None)
    return jax.shard_map(
        local,
        mesh=grid,
        in_specs=(shards, shards, shards, tokens, tokens, tokens, P(), P(), P()),
        out_specs=(tokens, shards, shards, shards),
        check_vma=False,
    )
```

time: 366 us -> 199 us (0.54)
  waiting for transfers between devices: 259 us -> 72.7 us
  Pallas kernels: 0 us -> 28.6 us
  starting transfers between devices: 39.4 us -> 60.2 us
  matrix products: 13.8 us -> 0 us
  other arithmetic: 8.89 us -> 2.03 us
  local copies, waits for them, and re-layouts: 10.1 us -> 3.93 us
    all_gather x2 -> x1, waiting for transfers between devices: 196 us -> 0.02 us  [local(): lax.all_gather(moved_weight, ('ring', 'near'), axis=0, tiled=False)]
    ppermute x0 -> x9, waiting for transfers between devices: none -> 51.4 us  [the longest x4 35.4 us: local(): up_sum = lax.ppermute(up_sum, 'ring', UP)]
    all_to_all x5, waiting for transfers between devices: 62.3 us -> 20.6 us  [the longest x1 19.4 us: local(): one = lax.all_to_all(one, TEAM, split_axis=0, concat_axis=0, tiled=True)]
    ppermute x0 -> x9, starting transfers between devices: none -> 36.4 us  [the longest x4 24.2 us: local(): down_sum = lax.ppermute(down_sum, 'ring', DOWN)]
    pallas_call x0 -> x9, Pallas kernels: none -> 28.6 us  [the longest x2 10 us: produce(): pl.pallas_call(functools.partial(produce_kernel, mate), out_shape=shape((...]
    all_to_all x5, starting transfers between devices: 39.3 us -> 23.8 us  [the longest x1 5.87 us: relocate(): lax.all_to_all(ordered, 'expert', split_axis=0, concat_axis=0, tiled=True)]
    dot_general x2 -> x0, matrix products: 13.8 us -> none  [the longest x1 7.15 us: local(): jnp.einsum('rf,rc->fc', shards, grad_columns, preferred_element_type=jnp....]
    reduce_sum x2 -> x0, other arithmetic: 3.88 us -> none  [the longest x1 3.09 us: local(): jnp.sum(jnp.where(picked[:, None, None], shards, jnp.zeros_like(shards)),...]
  transfers between devices with their start and end apart: 7 -> 15, of which waited for: 5 -> 8; matrix products, arithmetic and copies ran while one was open for 8% -> 1% of each run, Pallas kernels for 0% -> 12%
where the time goes in v1:
time: 199 us; the launch traced here: 197 us
  waiting for transfers between devices  72.7 us (37%)
  starting transfers between devices  60.2 us (30%)
  Pallas kernels  28.6 us (14%)
  blocking collectives  15.5 us (8%)
  between operations  14.4 us (7%)
  local copies, waits for them, and re-layouts  3.93 us (2%)
  other arithmetic  2.03 us (1%)
    ppermute x4, waiting for transfers between devices, local(): up_sum = lax.ppermute(up_sum, 'ring', UP)  35.4 us
    ppermute x4, starting transfers between devices, local(): down_sum = lax.ppermute(down_sum, 'ring', DOWN)  24.2 us
    all_to_all x1, waiting for transfers between devices, local(): one = lax.all_to_all(one, TEAM, split_axis=0, concat_axis=0, tiled=True)  19.4 us
    ppermute x4, waiting for transfers between devices, local(): down_sum = lax.ppermute(down_sum, 'ring', DOWN)  16 us
    all_to_all x1, blocking collectives, local(): lax.all_to_all(weight.reshape(hosts, block_rows, columns), 'expert', spli...  15.5 us
    ppermute x4, starting transfers between devices, local(): up_sum = lax.ppermute(up_sum, 'ring', UP)  10.3 us
    pallas_call x2, Pallas kernels, produce(): pl.pallas_call(functools.partial(produce_kernel, mate), out_shape=shape((...  10 us
    all_to_all x1, starting transfers between devices, relocate(): lax.all_to_all(ordered, 'expert', split_axis=0, concat_axis=0, tiled=True)  5.87 us
  transfers between devices with their start and end apart: 15, of which 8 were waited for; matrix products, arithmetic and copies ran while one was open for 1% of the time, Pallas kernels for 12%

profile of v1, /device:TPU:6, one launch (start us, length us, event | category | flops | bytes accessed | tf_op | source)
XLA Modules:
  0.0 197.2 jit_solution(12425269460547814964)
XLA Ops:
  7.2 15.5 %all_to_all.30.value = bf16[16,64,128]{2,1,0:T(8,128)(2,1)} all-to-all(bf16[16,64,128]{2,1,0:T(8,128)(2,1)} %bitcast.18), channel_id=1, replica_groups=mesh['ring'=8,'near'=2,'half'=2,'expert'=16] {'expert'}, dimensions={0} | all-to-all | bytes 524288 | tf_op jit(solution)/shard_map/all_to_all | solution.py:245
  24.3 5.8 %all-to-all-start.2 = ((bf16[16,64,128]{2,1,0:T(8,128)(2,1)}), bf16[16,64,128]{2,1,0:T(8,128)(2,1)S(1)}, u32[]{:S(2)}, u32[]{:S(2)}) async-start(bf16[16,64,128]{2,1,0:T(8,128)(2,1)} %reorder.2.after), calls=%async_computation.2 | async-start | bytes 524288 | tf_op jit(solution)/shard_map/all_to_all | solution.py:249
  31.4 3.2 %prepare.1 = (bf16[4,11,128,128]{3,2,1,0:T(8,128)(2,1)}, bf16[4,5,128,128]{3,2,1,0:T(8,128)(2,1)}) custom-call(s32[3]{0:T(128)} %compare_select_fusion.1.place, s32[16]{0:T(128)} %new_host.5, s32[32,16]{1,0:T(8,128)} %copy.14.counts, bf16[128,1024]{1,0:T(8,128)(2,1)} %bitcast.19, bf16[128,1024]{1,0:T(8,128)(2,1)} %bitcast.20, bf16[128,4096]{1,0:T(8,128)(2,1)} %bitcast.15), custom_call_target="tpu_custom_call" | custom-call | bytes 3145728 | tf_op jit(solution)/shard_map/prepare/pallas_call | solution.py:60
  36.4 3.5 %all-to-all-start = ((bf16[4,11,128,128]{3,2,1,0:T(8,128)(2,1)}), bf16[4,11,128,128]{3,2,1,0:T(8,128)(2,1)S(1)}, u32[]{:S(2)}, u32[]{:S(2)}) async-start(bf16[4,11,128,128]{3,2,1,0:T(8,128)(2,1)} %get-tuple-element.23), calls=%async_computation | async-start | bytes 2883584 | tf_op jit(solution)/shard_map/all_to_all | solution.py:243
  40.7 19.4 %all-to-all-done.blocks = bf16[4,11,128,128]{3,2,1,0:T(8,128)(2,1)S(1)} async-done(((bf16[4,11,128,128]{3,2,1,0:T(8,128)(2,1)}), bf16[4,11,128,128]{3,2,1,0:T(8,128)(2,1)S(1)}, u32[]{:S(2)}, u32[]{:S(2)}) %all-to-all-start) | async-done | bytes 1441824 | tf_op jit(solution)/shard_map/all_to_all | solution.py:243
  60.2 3.7 %all-to-all-start.3 = ((bf16[4,5,128,128]{3,2,1,0:T(8,128)(2,1)}), bf16[4,5,128,128]{3,2,1,0:T(8,128)(2,1)S(1)}, u32[]{:S(2)}, u32[]{:S(2)}) async-start(bf16[4,5,128,128]{3,2,1,0:T(8,128)(2,1)} %get-tuple-element.28), calls=%async_computation.3 | async-start | bytes 1310720 | tf_op jit(solution)/shard_map/all_to_all | solution.py:244
  63.9 2.9 %first_parts.1 = (bf16[512,1024]{1,0:T(8,128)(2,1)}, bf16[64,1024]{1,0:T(8,128)(2,1)}, bf16[64,1024]{1,0:T(8,128)(2,1)}, bf16[128,1024]{1,0:T(8,128)(2,1)}, bf16[128,1024]{1,0:T(8,128)(2,1)}) custom-call(bf16[4,11,128,128]{3,2,1,0:T(8,128)(2,1)} %copy-done, bf16[16,64,128]{2,1,0:T(8,128)(2,1)} %reorder.2.after), custom_call_target="tpu_custom_call" | custom-call | flops 268435456 | bytes 3145728 | tf_op jit(solution)/shard_map/first_parts/pallas_call | solution.py:96
  66.8 3.0 %collective-permute-start.1 = (bf16[64,1024]{1,0:T(8,128)(2,1)}, bf16[64,1024]{1,0:T(8,128)(2,1)S(1)}, u32[]{:S(2)}, u32[]{:S(2)}) collective-permute-start(bf16[64,1024]{1,0:T(8,128)(2,1)} %get-tuple-element.25), channel_id=1, source_target_pairs={{0,64},{64,128},{128,192},{192,256},{256,320},{320,384},{384,448},... | collective-permute-start | bytes 393224 | tf_op jit(solution)/shard_map/ppermute | solution.py:260
  70.9 23.2 %collective-permute-done.1 = bf16[64,1024]{1,0:T(8,128)(2,1)S(1)} collective-permute-done((bf16[64,1024]{1,0:T(8,128)(2,1)}, bf16[64,1024]{1,0:T(8,128)(2,1)S(1)}, u32[]{:S(2)}, u32[]{:S(2)}) %collective-permute-start.1) | collective-permute-done | bytes 131104 | tf_op jit(solution)/shard_map/ppermute | solution.py:260
  94.2 4.8 %all-to-all-start.4 = ((f32[16,128,128]{2,1,0:T(8,128)}), f32[16,128,128]{2,1,0:T(8,128)S(1)}, u32[]{:S(2)}, u32[]{:S(2)}) async-start(f32[16,128,128]{2,1,0:T(8,128)} %pad_maximum_fusion), calls=%async_computation.4 | async-start | bytes 2097152 | tf_op jit(solution)/shard_map/all_to_all | solution.py:170
  99.0 3.8 %collective-permute-start.5 = (bf16[64,1024]{1,0:T(8,128)(2,1)S(1)}, bf16[64,1024]{1,0:T(8,128)(2,1)S(1)}, u32[]{:S(2)}, u32[]{:S(2)}) collective-permute-start(bf16[64,1024]{1,0:T(8,128)(2,1)S(1)} %copy-done.17), channel_id=1, source_target_pairs={{0,448},{64,0},{128,64},{192,128},{256,192},{320,256},{384,320},{4... | collective-permute-start | bytes 393224 | tf_op jit(solution)/shard_map/ppermute | solution.py:261
  102.9 6.4 %collective-permute-done.5 = bf16[64,1024]{1,0:T(8,128)(2,1)S(1)} collective-permute-done((bf16[64,1024]{1,0:T(8,128)(2,1)S(1)}, bf16[64,1024]{1,0:T(8,128)(2,1)S(1)}, u32[]{:S(2)}, u32[]{:S(2)}) %collective-permute-start.5) | collective-permute-done | bytes 131104 | tf_op jit(solution)/shard_map/ppermute | solution.py:261
  109.4 6.5 %collective-permute-start.6 = (bf16[128,1024]{1,0:T(8,128)(2,1)S(1)}, bf16[128,1024]{1,0:T(8,128)(2,1)S(1)}, u32[]{:S(2)}, u32[]{:S(2)}) collective-permute-start(bf16[128,1024]{1,0:T(8,128)(2,1)S(1)} %pad_maximum_fusion.2), channel_id=1, source_target_pairs={{0,448},{64,0},{128,64},{192,128},{256,192},{320,256},{384,320},{4... | collective-permute-start | bytes 786440 | tf_op jit(solution)/shard_map/ppermute | solution.py:261
  115.9 3.0 %second_parts.1 = (bf16[128,1024]{1,0:T(8,128)(2,1)}, bf16[128,1024]{1,0:T(8,128)(2,1)}, bf16[128,1024]{1,0:T(8,128)(2,1)}, bf16[128,1024]{1,0:T(8,128)(2,1)}, bf16[128,1024]{1,0:T(8,128)(2,1)}) custom-call(bf16[4,5,128,128]{3,2,1,0:T(8,128)(2,1)} %copy-done.4, bf16[512,1024]{1,0:T(8,128)(2,1)} %get-tuple-element.24.rows), custom_call_target="tpu_custom_call" | custom-call | flops 536870912 | bytes 3145728 | tf_op jit(solution)/shard_map/second_parts/pallas_call | solution.py:114
  124.1 5.9 %all-to-all-start.5 = ((f32[16,128,128]{2,1,0:T(8,128)}), f32[16,128,128]{2,1,0:T(8,128)S(1)}, u32[]{:S(2)}, u32[]{:S(2)}) async-start(f32[16,128,128]{2,1,0:T(8,128)} %reorder.3), calls=%async_computation.5 | async-start | bytes 2097152 | tf_op jit(solution)/shard_map/all_to_all | solution.py:172
  131.0 6.5 %collective-permute-start.7 = (bf16[128,1024]{1,0:T(8,128)(2,1)S(1)}, bf16[128,1024]{1,0:T(8,128)(2,1)S(1)}, u32[]{:S(2)}, u32[]{:S(2)}) collective-permute-start(bf16[128,1024]{1,0:T(8,128)(2,1)S(1)} %add_convert_fusion.1), channel_id=1, source_target_pairs={{0,448},{64,0},{128,64},{192,128},{256,192},{320,256},{384,320},{4... | collective-permute-start | bytes 786440 | tf_op jit(solution)/shard_map/ppermute | solution.py:261
  138.1 3.5 %collective-permute-start.3 = (bf16[128,1024]{1,0:T(8,128)(2,1)S(1)}, bf16[128,1024]{1,0:T(8,128)(2,1)S(1)}, u32[]{:S(2)}, u32[]{:S(2)}) collective-permute-start(bf16[128,1024]{1,0:T(8,128)(2,1)S(1)} %add_convert_fusion.3), channel_id=1, source_target_pairs={{0,64},{64,128},{128,192},{192,256},{256,320},{320,384},{384,448},... | collective-permute-start | bytes 786440 | tf_op jit(solution)/shard_map/ppermute | solution.py:260
  141.6 8.7 %collective-permute-done.7 = bf16[128,1024]{1,0:T(8,128)(2,1)S(1)} collective-permute-done((bf16[128,1024]{1,0:T(8,128)(2,1)S(1)}, bf16[128,1024]{1,0:T(8,128)(2,1)S(1)}, u32[]{:S(2)}, u32[]{:S(2)}) %collective-permute-start.7) | collective-permute-done | bytes 262176 | tf_op jit(solution)/shard_map/ppermute | solution.py:261
  150.4 7.4 %collective-permute-start.8 = (bf16[128,1024]{1,0:T(8,128)(2,1)S(1)}, bf16[128,1024]{1,0:T(8,128)(2,1)S(1)}, u32[]{:S(2)}, u32[]{:S(2)}) collective-permute-start(bf16[128,1024]{1,0:T(8,128)(2,1)S(1)} %add_convert_fusion), channel_id=1, source_target_pairs={{0,448},{64,0},{128,64},{192,128},{256,192},{320,256},{384,320},{4... | collective-permute-start | bytes 786440 | tf_op jit(solution)/shard_map/ppermute | solution.py:261
  157.8 5.0 %produce.3 = bf16[16,128,128]{2,1,0:T(8,128)(2,1)} custom-call(s32[3]{0:T(128)} %compare_select_fusion.1.place, bf16[512,1024]{1,0:T(8,128)(2,1)} %get-tuple-element.24.rows, bf16[16,1024,128]{2,1,0:T(8,128)(2,1)} %all-gather.2.cloned.1.call-done.blocks), custom_call_target="tpu_custom_call" | custom-call | flops 536870912 | bytes 5242880 | tf_op jit(solution)/shard_map/produce/pallas_call | solution.py:137
  166.8 11.6 %collective-permute-done.4.rising = bf16[128,1024]{1,0:T(8,128)(2,1)S(1)} collective-permute-done((bf16[128,1024]{1,0:T(8,128)(2,1)S(1)}, bf16[128,1024]{1,0:T(8,128)(2,1)S(1)}, u32[]{:S(2)}, u32[]{:S(2)}) %collective-permute-start.4) | collective-permute-done | bytes 262176 | tf_op jit(solution)/shard_map/ppermute | solution.py:260
  179.1 3.0 %adam.1 = (bf16[1024,128]{1,0:T(8,128)(2,1)}, f32[1024,128]{1,0:T(8,128)}, f32[1024,128]{1,0:T(8,128)}) custom-call(bf16[1024,128]{1,0:T(8,128)(2,1)} %bitcast.13, f32[16,128,128]{2,1,0:T(8,128)} %copy-done.1, bf16[128,1024]{1,0:T(8,128)(2,1)} %get-tuple-element.33.part, bf16[128,1024]{1,0:T(8,128)(2,1)} %copy-done.15, bf16[128,1024]{1,0:T(8,128)(2,1)} %copy-done.14), custom_call_target="tpu_custom_call" | custom-call | bytes 3145728 | tf_op jit(solution)/shard_map/adam/pallas_call | solution.py:213
  182.1 5.0 %produce.2.near = bf16[16,128,128]{2,1,0:T(8,128)(2,1)} custom-call(s32[3]{0:T(128)} %compare_select_fusion.1.place, bf16[512,1024]{1,0:T(8,128)(2,1)} %get-tuple-element.24.rows, bf16[16,1024,128]{2,1,0:T(8,128)(2,1)} %all-gather.2.cloned.1.call-done.blocks), custom_call_target="tpu_custom_call" | custom-call | flops 536870912 | bytes 5242880 | tf_op jit(solution)/shard_map/produce/pallas_call | solution.py:137
  187.9 2.5 %assemble.1 = bf16[128,4096]{1,0:T(8,128)(2,1)} custom-call(s32[3]{0:T(128)} %compare_select_fusion.1.place, bf16[16,128,128]{2,1,0:T(8,128)(2,1)} %produce.2.near, bf16[16,128,128]{2,1,0:T(8,128)(2,1)} %copy-done.5), custom_call_target="tpu_custom_call" | custom-call | bytes 2097152 | tf_op jit(solution)/shard_map/assemble/pallas_call | solution.py:184
  (66 shorter events, 19.0 us)
Async XLA Ops:
  7.2 23.0 %copy-start.16 = (s32[32,16]{0,1:T(8,128)S(1)}, s32[32,16]{0,1:T(8,128)}, u32[]{:S(2)}) copy-start(s32[32,16]{0,1:T(8,128)} %param.17) | copy-start | bytes 6148
  24.3 11.4 %all-to-all-start.2 = ((bf16[16,64,128]{2,1,0:T(8,128)(2,1)}), bf16[16,64,128]{2,1,0:T(8,128)(2,1)S(1)}, u32[]{:S(2)}, u32[]{:S(2)}) async-start(bf16[16,64,128]{2,1,0:T(8,128)(2,1)} %reorder.2.after), calls=%async_computation.2 | async-start | bytes 524288 | tf_op jit(solution)/shard_map/all_to_all | solution.py:249
  36.4 23.7 %all-to-all-start = ((bf16[4,11,128,128]{3,2,1,0:T(8,128)(2,1)}), bf16[4,11,128,128]{3,2,1,0:T(8,128)(2,1)S(1)}, u32[]{:S(2)}, u32[]{:S(2)}) async-start(bf16[4,11,128,128]{3,2,1,0:T(8,128)(2,1)} %get-tuple-element.23), calls=%async_computation | async-start | bytes 2883584 | tf_op jit(solution)/shard_map/all_to_all | solution.py:243
  40.0 117.8 %all-gather.2.cloned.1.call-start = ((), (), s32[]{:S(2)}) async-start(), calls=%async_computation.6 | async-start | bytes 4456448 | tf_op jit(solution)/shard_map/all_gather | solution.py:254
  60.2 34.0 %all-to-all-start.3 = ((bf16[4,5,128,128]{3,2,1,0:T(8,128)(2,1)}), bf16[4,5,128,128]{3,2,1,0:T(8,128)(2,1)S(1)}, u32[]{:S(2)}, u32[]{:S(2)}) async-start(bf16[4,5,128,128]{3,2,1,0:T(8,128)(2,1)} %get-tuple-element.28), calls=%async_computation.3 | async-start | bytes 1310720 | tf_op jit(solution)/shard_map/all_to_all | solution.py:244
  66.8 27.3 %collective-permute-start.1 = (bf16[64,1024]{1,0:T(8,128)(2,1)}, bf16[64,1024]{1,0:T(8,128)(2,1)S(1)}, u32[]{:S(2)}, u32[]{:S(2)}) collective-permute-start(bf16[64,1024]{1,0:T(8,128)(2,1)} %get-tuple-element.25), channel_id=1, source_target_pairs={{0,64},{64,128},{128,192},{192,256},{256,320},{320,384},{384,448},... | collective-permute-start | bytes 393224 | tf_op jit(solution)/shard_map/ppermute | solution.py:260
  70.9 28.1 %copy-start.17 = (bf16[64,1024]{1,0:T(8,128)(2,1)S(1)}, bf16[64,1024]{1,0:T(8,128)(2,1)}, u32[]{:S(2)}) copy-start(bf16[64,1024]{1,0:T(8,128)(2,1)} %get-tuple-element.36) | copy-start | bytes 393220
  70.9 31.9 %copy-start.12 = (bf16[128,1024]{1,0:T(8,128)(2,1)S(1)}, bf16[128,1024]{1,0:T(8,128)(2,1)}, u32[]{:S(2)}) copy-start(bf16[128,1024]{1,0:T(8,128)(2,1)} %get-tuple-element.35) | copy-start | bytes 786436
  94.2 15.1 %copy-start.4 = (bf16[4,5,128,128]{3,2,1,0:T(8,128)(2,1)}, bf16[4,5,128,128]{3,2,1,0:T(8,128)(2,1)S(1)}, u32[]{:S(2)}) copy-start(bf16[4,5,128,128]{3,2,1,0:T(8,128)(2,1)S(1)} %all-to-all-done.3.blocks) | copy-start | bytes 1966084
  94.2 26.6 %all-to-all-start.4 = ((f32[16,128,128]{2,1,0:T(8,128)}), f32[16,128,128]{2,1,0:T(8,128)S(1)}, u32[]{:S(2)}, u32[]{:S(2)}) async-start(f32[16,128,128]{2,1,0:T(8,128)} %pad_maximum_fusion), calls=%async_computation.4 | async-start | bytes 2097152 | tf_op jit(solution)/shard_map/all_to_all | solution.py:170
  99.0 10.3 %collective-permute-start.5 = (bf16[64,1024]{1,0:T(8,128)(2,1)S(1)}, bf16[64,1024]{1,0:T(8,128)(2,1)S(1)}, u32[]{:S(2)}, u32[]{:S(2)}) collective-permute-start(bf16[64,1024]{1,0:T(8,128)(2,1)S(1)} %copy-done.17), channel_id=1, source_target_pairs={{0,448},{64,0},{128,64},{192,128},{256,192},{320,256},{384,320},{4... | collective-permute-start | bytes 393224 | tf_op jit(solution)/shard_map/ppermute | solution.py:261
  109.4 21.6 %collective-permute-start.6 = (bf16[128,1024]{1,0:T(8,128)(2,1)S(1)}, bf16[128,1024]{1,0:T(8,128)(2,1)S(1)}, u32[]{:S(2)}, u32[]{:S(2)}) collective-permute-start(bf16[128,1024]{1,0:T(8,128)(2,1)S(1)} %pad_maximum_fusion.2), channel_id=1, source_target_pairs={{0,448},{64,0},{128,64},{192,128},{256,192},{320,256},{384,320},{4... | collective-permute-start | bytes 786440 | tf_op jit(solution)/shard_map/ppermute | solution.py:261
  118.9 19.2 %collective-permute-start.2 = (bf16[128,1024]{1,0:T(8,128)(2,1)S(1)}, bf16[128,1024]{1,0:T(8,128)(2,1)S(1)}, u32[]{:S(2)}, u32[]{:S(2)}) collective-permute-start(bf16[128,1024]{1,0:T(8,128)(2,1)S(1)} %pad_maximum_fusion.1), channel_id=1, source_target_pairs={{0,64},{64,128},{128,192},{192,256},{256,320},{320,384},{384,448},... | collective-permute-start | bytes 786440 | tf_op jit(solution)/shard_map/ppermute | solution.py:260
  124.1 13.9 %copy-start.10 = (bf16[128,1024]{1,0:T(8,128)(2,1)S(1)}, bf16[128,1024]{1,0:T(8,128)(2,1)}, u32[]{:S(2)}) copy-start(bf16[128,1024]{1,0:T(8,128)(2,1)} %get-tuple-element.29) | copy-start | bytes 786436
  124.1 26.2 %copy-start.9 = (bf16[128,1024]{1,0:T(8,128)(2,1)S(1)}, bf16[128,1024]{1,0:T(8,128)(2,1)}, u32[]{:S(2)}) copy-start(bf16[128,1024]{1,0:T(8,128)(2,1)} %get-tuple-element.38) | copy-start | bytes 786436
  124.1 40.7 %all-to-all-start.5 = ((f32[16,128,128]{2,1,0:T(8,128)}), f32[16,128,128]{2,1,0:T(8,128)S(1)}, u32[]{:S(2)}, u32[]{:S(2)}) async-start(f32[16,128,128]{2,1,0:T(8,128)} %reorder.3), calls=%async_computation.5 | async-start | bytes 2097152 | tf_op jit(solution)/shard_map/all_to_all | solution.py:172
  131.0 19.3 %collective-permute-start.7 = (bf16[128,1024]{1,0:T(8,128)(2,1)S(1)}, bf16[128,1024]{1,0:T(8,128)(2,1)S(1)}, u32[]{:S(2)}, u32[]{:S(2)}) collective-permute-start(bf16[128,1024]{1,0:T(8,128)(2,1)S(1)} %add_convert_fusion.1), channel_id=1, source_target_pairs={{0,448},{64,0},{128,64},{192,128},{256,192},{320,256},{384,320},{4... | collective-permute-start | bytes 786440 | tf_op jit(solution)/shard_map/ppermute | solution.py:261
  138.1 26.6 %collective-permute-start.3 = (bf16[128,1024]{1,0:T(8,128)(2,1)S(1)}, bf16[128,1024]{1,0:T(8,128)(2,1)S(1)}, u32[]{:S(2)}, u32[]{:S(2)}) collective-permute-start(bf16[128,1024]{1,0:T(8,128)(2,1)S(1)} %add_convert_fusion.3), channel_id=1, source_target_pairs={{0,64},{64,128},{128,192},{192,256},{256,320},{320,384},{384,448},... | collective-permute-start | bytes 786440 | tf_op jit(solution)/shard_map/ppermute | solution.py:260
  150.4 14.4 %copy-start.8 = (bf16[128,1024]{1,0:T(8,128)(2,1)S(1)}, bf16[128,1024]{1,0:T(8,128)(2,1)}, u32[]{:S(2)}) copy-start(bf16[128,1024]{1,0:T(8,128)(2,1)} %get-tuple-element.30) | copy-start | bytes 786436
  150.4 16.4 %collective-permute-start.8 = (bf16[128,1024]{1,0:T(8,128)(2,1)S(1)}, bf16[128,1024]{1,0:T(8,128)(2,1)S(1)}, u32[]{:S(2)}, u32[]{:S(2)}) collective-permute-start(bf16[128,1024]{1,0:T(8,128)(2,1)S(1)} %add_convert_fusion), channel_id=1, source_target_pairs={{0,448},{64,0},{128,64},{192,128},{256,192},{320,256},{384,320},{4... | collective-permute-start | bytes 786440 | tf_op jit(solution)/shard_map/ppermute | solution.py:261
  162.8 24.3 %collective-permute-start = (bf16[16,128,128]{2,1,0:T(8,128)(2,1)}, bf16[16,128,128]{2,1,0:T(8,128)(2,1)S(1)}, u32[]{:S(2)}, u32[]{:S(2)}) collective-permute-start(bf16[16,128,128]{2,1,0:T(8,128)(2,1)} %produce.3), channel_id=1, source_target_pairs={{0,16},{16,0},{1,17},{17,1},{2,18},{18,2},{3,19},{19,3},{4,20},{20... | collective-permute-start | bytes 1572872 | tf_op jit(solution)/shard_map/ppermute | solution.py:255
  164.8 13.6 %copy-start.1 = (f32[16,128,128]{2,1,0:T(8,128)}, f32[16,128,128]{2,1,0:T(8,128)S(1)}, u32[]{:S(2)}) copy-start(f32[16,128,128]{2,1,0:T(8,128)S(1)} %all-to-all-done.5.moments) | copy-start | bytes 3145732
  164.8 13.6 %collective-permute-start.4 = (bf16[128,1024]{1,0:T(8,128)(2,1)S(1)}, bf16[128,1024]{1,0:T(8,128)(2,1)S(1)}, u32[]{:S(2)}, u32[]{:S(2)}) collective-permute-start(bf16[128,1024]{1,0:T(8,128)(2,1)S(1)} %add_convert_fusion.2), channel_id=1, source_target_pairs={{0,64},{64,128},{128,192},{192,256},{256,320},{320,384},{384,448},... | collective-permute-start | bytes 786440 | tf_op jit(solution)/shard_map/ppermute | solution.py:260
  166.8 11.6 %copy-start.14 = (bf16[128,1024]{1,0:T(8,128)(2,1)}, bf16[128,1024]{1,0:T(8,128)(2,1)S(1)}, u32[]{:S(2)}) copy-start(bf16[128,1024]{1,0:T(8,128)(2,1)S(1)} %collective-permute-done.8.falling) | copy-start | bytes 786436
  (9 other events, 37.1 us)
Sparse Core Ops, SparseCore 0:
  42.9 105.3 all-gather.1

commit v2 on v1

--- a/solution.py
+++ b/solution.py
@@ -121,7 +121,8 @@
     )(blocks, rows)
 
 
-def produce_kernel(mate, place, rows, blocks, out):
+def produce_kernel(mate, place, rows, blocks, *refs):
+    out = refs[-1]
     member = place[1]
     if mate:
         member = member + 1 - 2 * lax.rem(member, 2)
@@ -131,7 +132,7 @@
         out[i] = jnp.dot(mine, blocks[i], preferred_element_type=jnp.float32).astype(out.dtype)
 
 
-def produce(mate, place, rows, blocks):
+def produce(mate, place, rows, blocks, after):
     count, hidden_units, columns = blocks.shape
     size, step = rows.shape[0] // 4, 4
     return pl.pallas_call(
@@ -142,11 +143,12 @@
             SMEM,
             pl.BlockSpec(rows.shape, lambda i: (0, 0)),
             pl.BlockSpec((step, hidden_units, columns), lambda i: (i, 0, 0)),
-        ],
+        ]
+        + [ANY] * len(after),
         out_specs=pl.BlockSpec((step, size, columns), lambda i: (i, 0, 0)),
         cost_estimate=cost(count << 25, 5 << 20),
         name="produce",
-    )(place, rows, blocks)
+    )(place, rows, blocks, *after)
 
 
 def reorder_kernel(old_host, new_host, value, *refs):
@@ -166,12 +168,6 @@
     )(old_host, new_host, value, *after)
 
 
-def relocate(blocks, old_host, new_host, *after):
-    spread = lax.all_to_all(blocks, "expert", split_axis=0, concat_axis=0, tiled=True)
-    ordered = reorder(spread, old_host, new_host, after)
-    return lax.all_to_all(ordered, "expert", split_axis=0, concat_axis=0, tiled=True)
-
-
 def assemble_kernel(place, near, far, out):
     half = lax.rem(place[1], 2)
     for owner in range(N_Z):
@@ -191,7 +187,7 @@
     )(place, near, far)
 
 
-def adam_kernel(weight, moments, part, rising, falling, new_weight, new_first, new_second):
+def adam_kernel(weight, moments, part, rising, falling, after, new_weight, new_first, new_second):
     hosts, both, _ = moments.shape
     step = both // 2
     grad = part[...].astype(jnp.float32) + rising[...].astype(jnp.float32)
@@ -209,7 +205,7 @@
         new_weight[at] = (weight[at].astype(jnp.float32) - update).astype(new_weight.dtype)
 
 
-def adam(weight, moments, part, rising, falling):
+def adam(weight, moments, part, rising, falling, after):
     return pl.pallas_call(
         adam_kernel,
         out_shape=[
@@ -217,11 +213,11 @@
             shape(weight.shape, jnp.float32),
             shape(weight.shape, jnp.float32),
         ],
-        in_specs=[VMEM] * 5,
+        in_specs=[VMEM] * 5 + [ANY],
         out_specs=[VMEM] * 3,
         cost_estimate=cost(0, 3 << 20),
         name="adam",
-    )(weight, moments, part, rising, falling)
+    )(weight, moments, part, rising, falling, after)
 
 
 def add(left, right):
@@ -240,23 +236,33 @@
     half = columns // 2
 
     one, two = prepare(place, new_host, counts, gate_act[0], up_act[0], out_grad[0])
+    order = two
     one = lax.all_to_all(one, TEAM, split_axis=0, concat_axis=0, tiled=True)
     two = lax.all_to_all(two, TEAM, split_axis=0, concat_axis=0, tiled=True)
     spread = lax.all_to_all(
         weight.reshape(hosts, block_rows, columns), "expert", split_axis=0, concat_axis=0, tiled=True
     )
-    ordered = reorder(spread, old_host, new_host, [])
+    ordered = reorder(spread, old_host, new_host, [order])
     moved_weight = lax.all_to_all(ordered, "expert", split_axis=0, concat_axis=0, tiled=True)
     moved_weight = moved_weight.reshape(hidden_units, columns)
-    rows, low, high, *part = first_parts(one, ordered)
+    rows, low, high, *part = first_parts(one, order)
     part = dict(zip(FIRST[1:] + SECOND, [*part, *second_parts(two, rows)]))
 
     gathered = lax.all_gather(moved_weight, ("ring", "near"), axis=0, tiled=False)
-    far = lax.ppermute(produce(True, place, rows, gathered), "half", SWAP)
-    output = assemble(place, produce(False, place, rows, gathered), far)
-
     up_sum, down_sum = low, high
+    stacked = jnp.concatenate(
+        [
+            first_moment.reshape(hosts, block_rows, columns),
+            second_moment.reshape(hosts, block_rows, columns),
+        ],
+        axis=1,
+    )
+    stacked, part[0] = lax.optimization_barrier((stacked, part[0]))
+    spread = lax.all_to_all(stacked, "expert", split_axis=0, concat_axis=0, tiled=True)
+    ordered = reorder(spread, old_host, new_host, [])
+    moments = lax.all_to_all(ordered, "expert", split_axis=0, concat_axis=0, tiled=True)
     for step in range(1, N_FAR // 2 + 1):
+        last = [up_sum, down_sum]
         up_sum = lax.ppermute(up_sum, "ring", UP)
         down_sum = lax.ppermute(down_sum, "ring", DOWN)
         if step < N_FAR // 2:
@@ -266,19 +272,10 @@
                 down_sum = jnp.concatenate([down_part[:half], add(down_sum, down_part[half:])])
             else:
                 up_sum, down_sum = add(up_sum, up_part), add(down_sum, down_part)
-        if step == 1:
-            stacked = jnp.concatenate(
-                [
-                    first_moment.reshape(hosts, block_rows, columns),
-                    second_moment.reshape(hosts, block_rows, columns),
-                ],
-                axis=1,
-            )
-            stacked, up_sum = lax.optimization_barrier((stacked, up_sum))
-            moments = relocate(stacked, old_host, new_host)
-        if step == 3:
-            up_sum, moments = lax.optimization_barrier((up_sum, moments))
-    new_weight, new_first, new_second = adam(moved_weight, moments, part[0], up_sum, down_sum)
+    far = lax.ppermute(produce(True, place, rows, gathered, last), "half", SWAP)
+    near = produce(False, place, rows, gathered, [])
+    output = assemble(place, near, far)
+    new_weight, new_first, new_second = adam(moved_weight, moments, part[0], up_sum, down_sum, near)
     return (output[None], new_weight[None], new_first[None], new_second[None])
 
 

time: 199 us -> 193 us (0.970)
  the two profiles are of different devices: /device:TPU:6 before, /device:TPU:38 now
where the time goes in v2:
time: 193 us; the launch traced here: 192 us
  starting transfers between devices  74 us (38%)
  waiting for transfers between devices  54 us (28%)
  Pallas kernels  28.6 us (15%)
  between operations  14.3 us (7%)
  blocking collectives  12 us (6%)
  local copies, waits for them, and re-layouts  5.82 us (3%)
  other arithmetic  3.37 us (2%)
    ppermute x4, starting transfers between devices, local(): down_sum = lax.ppermute(down_sum, 'ring', DOWN)  25.3 us
    ppermute x4, waiting for transfers between devices, local(): up_sum = lax.ppermute(up_sum, 'ring', UP)  21.2 us
    all_to_all x1, waiting for transfers between devices, local(): one = lax.all_to_all(one, TEAM, split_axis=0, concat_axis=0, tiled=True)  18.9 us
    ppermute x4, starting transfers between devices, local(): up_sum = lax.ppermute(up_sum, 'ring', UP)  15 us
    all_to_all x1, blocking collectives, local(): lax.all_to_all(ordered, 'expert', split_axis=0, concat_axis=0, tiled=True)  12 us
    pallas_call x2, Pallas kernels, produce(): pl.pallas_call(functools.partial(produce_kernel, mate), out_shape=shape((...  10 us
    all_to_all x1, starting transfers between devices, local(): one = lax.all_to_all(one, TEAM, split_axis=0, concat_axis=0, tiled=True)  7.08 us
    all_gather x1, waiting for transfers between devices, local(): lax.all_gather(moved_weight, ('ring', 'near'), axis=0, tiled=False)  6.36 us
  transfers between devices with their start and end apart: 15, of which 9 were waited for; matrix products, arithmetic and copies ran while one was open for 2% of the time, Pallas kernels for 13%

profile of v2, /device:TPU:38, one launch (start us, length us, event | category | flops | bytes accessed | tf_op | source)
XLA Modules:
  0.0 192.1 jit_solution(15878047654088706660)
XLA Ops:
  7.2 5.8 %all-to-all-start.1 = ((bf16[16,64,128]{2,1,0:T(8,128)(2,1)}), bf16[16,64,128]{2,1,0:T(8,128)(2,1)S(1)}, u32[]{:S(2)}, u32[]{:S(2)}) async-start(bf16[16,64,128]{2,1,0:T(8,128)(2,1)} %bitcast.18), calls=%async_computation.1 | async-start | bytes 524288 | tf_op jit(solution)/shard_map/all_to_all | solution.py:242
  14.9 3.2 %prepare.1 = (bf16[4,11,128,128]{3,2,1,0:T(8,128)(2,1)}, bf16[4,5,128,128]{3,2,1,0:T(8,128)(2,1)}) custom-call(s32[3]{0:T(128)} %compare_select_fusion.1.place, s32[16]{0:T(128)} %new_host.5, s32[32,16]{1,0:T(8,128)} %copy.14.counts, bf16[128,1024]{1,0:T(8,128)(2,1)} %bitcast.19, bf16[128,1024]{1,0:T(8,128)(2,1)} %bitcast.20, bf16[128,4096]{1,0:T(8,128)(2,1)} %bitcast.15), custom_call_target="tpu_custom_call" | custom-call | bytes 3145728 | tf_op jit(solution)/shard_map/prepare/pallas_call | solution.py:60
  20.9 12.0 %all_to_all.30 = bf16[16,64,128]{2,1,0:T(8,128)(2,1)} all-to-all(bf16[16,64,128]{2,1,0:T(8,128)(2,1)} %reorder.2), channel_id=1, replica_groups=mesh['ring'=8,'near'=2,'half'=2,'expert'=16] {'expert'}, dimensions={0} | all-to-all | bytes 524288 | tf_op jit(solution)/shard_map/all_to_all | solution.py:246
  33.0 7.1 %all-to-all-start = ((bf16[4,11,128,128]{3,2,1,0:T(8,128)(2,1)}), bf16[4,11,128,128]{3,2,1,0:T(8,128)(2,1)S(1)}, u32[]{:S(2)}, u32[]{:S(2)}) async-start(bf16[4,11,128,128]{3,2,1,0:T(8,128)(2,1)} %get-tuple-element.21), calls=%async_computation | async-start | bytes 2883584 | tf_op jit(solution)/shard_map/all_to_all | solution.py:240
  40.8 18.9 %all-to-all-done.blocks = bf16[4,11,128,128]{3,2,1,0:T(8,128)(2,1)S(1)} async-done(((bf16[4,11,128,128]{3,2,1,0:T(8,128)(2,1)}), bf16[4,11,128,128]{3,2,1,0:T(8,128)(2,1)S(1)}, u32[]{:S(2)}, u32[]{:S(2)}) %all-to-all-start) | async-done | bytes 1441824 | tf_op jit(solution)/shard_map/all_to_all | solution.py:240
  59.7 4.0 %all-to-all-start.3 = ((bf16[4,5,128,128]{3,2,1,0:T(8,128)(2,1)}), bf16[4,5,128,128]{3,2,1,0:T(8,128)(2,1)S(1)}, u32[]{:S(2)}, u32[]{:S(2)}) async-start(bf16[4,5,128,128]{3,2,1,0:T(8,128)(2,1)} %get-tuple-element.22.after.refs_0_), calls=%async_computation.3 | async-start | bytes 1310720 | tf_op jit(solution)/shard_map/all_to_all | solution.py:241
  66.6 3.6 %collective-permute-start = (bf16[64,1024]{1,0:T(8,128)(2,1)}, bf16[64,1024]{1,0:T(8,128)(2,1)S(1)}, u32[]{:S(2)}, u32[]{:S(2)}) collective-permute-start(bf16[64,1024]{1,0:T(8,128)(2,1)} %get-tuple-element.24), channel_id=1, source_target_pairs={{0,64},{64,128},{128,192},{192,256},{256,320},{320,384},{384,448},... | collective-permute-start | bytes 393224 | tf_op jit(solution)/shard_map/ppermute | solution.py:266
  71.3 7.7 %collective-permute-start.3 = (bf16[64,1024]{1,0:T(8,128)(2,1)S(1)}, bf16[64,1024]{1,0:T(8,128)(2,1)S(1)}, u32[]{:S(2)}, u32[]{:S(2)}) collective-permute-start(bf16[64,1024]{1,0:T(8,128)(2,1)S(1)} %copy-done.19), channel_id=1, source_target_pairs={{0,448},{64,0},{128,64},{192,128},{256,192},{320,256},{384,320},{4... | collective-permute-start | bytes 393224 | tf_op jit(solution)/shard_map/ppermute | solution.py:267
  80.7 3.0 %second_parts.1 = (bf16[128,1024]{1,0:T(8,128)(2,1)}, bf16[128,1024]{1,0:T(8,128)(2,1)}, bf16[128,1024]{1,0:T(8,128)(2,1)}, bf16[128,1024]{1,0:T(8,128)(2,1)}, bf16[128,1024]{1,0:T(8,128)(2,1)}) custom-call(bf16[4,5,128,128]{3,2,1,0:T(8,128)(2,1)} %copy-done.6, bf16[512,1024]{1,0:T(8,128)(2,1)} %get-tuple-element.23.rows), custom_call_target="tpu_custom_call" | custom-call | flops 536870912 | bytes 3145728 | tf_op jit(solution)/shard_map/second_parts/pallas_call | solution.py:114
  83.8 5.9 %all-to-all-start.4 = ((f32[16,128,128]{2,1,0:T(8,128)}), f32[16,128,128]{2,1,0:T(8,128)S(1)}, u32[]{:S(2)}, u32[]{:S(2)}) async-start(f32[16,128,128]{2,1,0:T(8,128)} %pad_maximum_fusion), calls=%async_computation.4 | async-start | bytes 2097152 | tf_op jit(solution)/shard_map/all_to_all | solution.py:261
  89.8 5.4 %collective-permute-start.1 = (bf16[128,1024]{1,0:T(8,128)(2,1)S(1)}, bf16[128,1024]{1,0:T(8,128)(2,1)S(1)}, u32[]{:S(2)}, u32[]{:S(2)}) collective-permute-start(bf16[128,1024]{1,0:T(8,128)(2,1)S(1)} %pad_maximum_fusion.1), channel_id=1, source_target_pairs={{0,64},{64,128},{128,192},{192,256},{256,320},{320,384},{384,448},... | collective-permute-start | bytes 786440 | tf_op jit(solution)/shard_map/ppermute | solution.py:266
  95.2 7.8 %collective-permute-start.4 = (bf16[128,1024]{1,0:T(8,128)(2,1)S(1)}, bf16[128,1024]{1,0:T(8,128)(2,1)S(1)}, u32[]{:S(2)}, u32[]{:S(2)}) collective-permute-start(bf16[128,1024]{1,0:T(8,128)(2,1)S(1)} %pad_maximum_fusion.2), channel_id=1, source_target_pairs={{0,448},{64,0},{128,64},{192,128},{256,192},{320,256},{384,320},{4... | collective-permute-start | bytes 786440 | tf_op jit(solution)/shard_map/ppermute | solution.py:267
  103.0 15.7 %collective-permute-done.1 = bf16[128,1024]{1,0:T(8,128)(2,1)S(1)} collective-permute-done((bf16[128,1024]{1,0:T(8,128)(2,1)S(1)}, bf16[128,1024]{1,0:T(8,128)(2,1)S(1)}, u32[]{:S(2)}, u32[]{:S(2)}) %collective-permute-start.1) | collective-permute-done | bytes 262176 | tf_op jit(solution)/shard_map/ppermute | solution.py:266
  120.9 6.0 %collective-permute-start.5 = (bf16[128,1024]{1,0:T(8,128)(2,1)S(1)}, bf16[128,1024]{1,0:T(8,128)(2,1)S(1)}, u32[]{:S(2)}, u32[]{:S(2)}) collective-permute-start(bf16[128,1024]{1,0:T(8,128)(2,1)S(1)} %add_convert_fusion.1), channel_id=1, source_target_pairs={{0,448},{64,0},{128,64},{192,128},{256,192},{320,256},{384,320},{4... | collective-permute-start | bytes 786440 | tf_op jit(solution)/shard_map/ppermute | solution.py:267
  130.2 5.9 %all-to-all-start.5 = ((f32[16,128,128]{2,1,0:T(8,128)}), f32[16,128,128]{2,1,0:T(8,128)S(1)}, u32[]{:S(2)}, u32[]{:S(2)}) async-start(f32[16,128,128]{2,1,0:T(8,128)} %reorder.3), calls=%async_computation.5 | async-start | bytes 2097152 | tf_op jit(solution)/shard_map/all_to_all | solution.py:263
  136.2 4.9 %collective-permute-done.2 = bf16[128,1024]{1,0:T(8,128)(2,1)S(1)} collective-permute-done((bf16[128,1024]{1,0:T(8,128)(2,1)S(1)}, bf16[128,1024]{1,0:T(8,128)(2,1)S(1)}, u32[]{:S(2)}, u32[]{:S(2)}) %collective-permute-start.2) | collective-permute-done | bytes 262176 | tf_op jit(solution)/shard_map/ppermute | solution.py:266
  143.2 6.4 %all-gather.2.cloned.1.call-done.blocks = bf16[16,1024,128]{2,1,0:T(8,128)(2,1)} async-done(((bf16[1,1024,128]{2,1,0:T(8,128)(2,1)}), bf16[16,1024,128]{2,1,0:T(8,128)(2,1)}) %all-gather.2.cloned.1.call-update) | async-done | bytes 4194320 | tf_op jit(solution)/shard_map/all_gather | solution.py:251
  149.5 5.0 %produce.3 = bf16[16,128,128]{2,1,0:T(8,128)(2,1)} custom-call(s32[3]{0:T(128)} %compare_select_fusion.1.place, bf16[512,1024]{1,0:T(8,128)(2,1)} %get-tuple-element.23.rows, bf16[16,1024,128]{2,1,0:T(8,128)(2,1)} %all-gather.2.cloned.1.call-done.blocks, bf16[128,1024]{1,0:T(8,128)(2,1)} %add_convert_fusion.2.refs_0_, bf16[128,1024]{1,0:T(8,128)(2,1)} %add_convert_fusion.refs_1_), custom_call_target="tpu_custom_call" | custom-call | flops 536870912 | bytes 5242880 | tf_op jit(solution)/shard_map/produce/pallas_call | solution.py:138
  154.6 5.0 %collective-permute-start.6 = (bf16[16,128,128]{2,1,0:T(8,128)(2,1)}, bf16[16,128,128]{2,1,0:T(8,128)(2,1)S(1)}, u32[]{:S(2)}, u32[]{:S(2)}) collective-permute-start(bf16[16,128,128]{2,1,0:T(8,128)(2,1)} %produce.3), channel_id=1, source_target_pairs={{0,16},{16,0},{1,17},{17,1},{2,18},{18,2},{3,19},{19,3},{4,20},{20... | collective-permute-start | bytes 1572872 | tf_op jit(solution)/shard_map/ppermute | solution.py:275
  159.5 4.2 %collective-permute-start.7 = (bf16[128,1024]{1,0:T(8,128)(2,1)S(1)}, bf16[128,1024]{1,0:T(8,128)(2,1)S(1)}, u32[]{:S(2)}, u32[]{:S(2)}) collective-permute-start(bf16[128,1024]{1,0:T(8,128)(2,1)S(1)} %copy-done.3), channel_id=1, source_target_pairs={{0,64},{64,128},{128,192},{192,256},{256,320},{320,384},{384,448},... | collective-permute-start | bytes 786440 | tf_op jit(solution)/shard_map/ppermute | solution.py:266
  163.7 3.8 %collective-permute-start.8 = (bf16[128,1024]{1,0:T(8,128)(2,1)S(1)}, bf16[128,1024]{1,0:T(8,128)(2,1)S(1)}, u32[]{:S(2)}, u32[]{:S(2)}) collective-permute-start(bf16[128,1024]{1,0:T(8,128)(2,1)S(1)} %copy-done.4), channel_id=1, source_target_pairs={{0,448},{64,0},{128,64},{192,128},{256,192},{320,256},{384,320},{4... | collective-permute-start | bytes 786440 | tf_op jit(solution)/shard_map/ppermute | solution.py:267
  167.5 5.0 %produce.2.near.after = bf16[16,128,128]{2,1,0:T(8,128)(2,1)} custom-call(s32[3]{0:T(128)} %compare_select_fusion.1.place, bf16[512,1024]{1,0:T(8,128)(2,1)} %get-tuple-element.23.rows, bf16[16,1024,128]{2,1,0:T(8,128)(2,1)} %all-gather.2.cloned.1.call-done.blocks), custom_call_target="tpu_custom_call" | custom-call | flops 536870912 | bytes 5242880 | tf_op jit(solution)/shard_map/produce/pallas_call | solution.py:138
  173.2 4.8 %collective-permute-done.8.falling = bf16[128,1024]{1,0:T(8,128)(2,1)S(1)} collective-permute-done((bf16[128,1024]{1,0:T(8,128)(2,1)S(1)}, bf16[128,1024]{1,0:T(8,128)(2,1)S(1)}, u32[]{:S(2)}, u32[]{:S(2)}) %collective-permute-start.8) | collective-permute-done | bytes 262176 | tf_op jit(solution)/shard_map/ppermute | solution.py:267
  179.0 3.0 %adam.1 = (bf16[1024,128]{1,0:T(8,128)(2,1)}, f32[1024,128]{1,0:T(8,128)}, f32[1024,128]{1,0:T(8,128)}) custom-call(bf16[1024,128]{1,0:T(8,128)(2,1)} %bitcast.13, f32[16,128,128]{2,1,0:T(8,128)} %copy-done.1, bf16[128,1024]{1,0:T(8,128)(2,1)} %get-tuple-element.34.part, bf16[128,1024]{1,0:T(8,128)(2,1)} %copy-done.14, bf16[128,1024]{1,0:T(8,128)(2,1)} %copy-done.15, ...), custom_call_target="tpu_custom_call" | custom-call | bytes 3145728 | tf_op jit(solution)/shard_map/adam/pallas_call | solution.py:209
  (70 shorter events, 23.7 us)
Async XLA Ops:
  7.2 11.4 %all-to-all-start.1 = ((bf16[16,64,128]{2,1,0:T(8,128)(2,1)}), bf16[16,64,128]{2,1,0:T(8,128)(2,1)S(1)}, u32[]{:S(2)}, u32[]{:S(2)}) async-start(bf16[16,64,128]{2,1,0:T(8,128)(2,1)} %bitcast.18), calls=%async_computation.1 | async-start | bytes 524288 | tf_op jit(solution)/shard_map/all_to_all | solution.py:242
  33.0 26.7 %all-to-all-start = ((bf16[4,11,128,128]{3,2,1,0:T(8,128)(2,1)}), bf16[4,11,128,128]{3,2,1,0:T(8,128)(2,1)S(1)}, u32[]{:S(2)}, u32[]{:S(2)}) async-start(bf16[4,11,128,128]{3,2,1,0:T(8,128)(2,1)} %get-tuple-element.21), calls=%async_computation | async-start | bytes 2883584 | tf_op jit(solution)/shard_map/all_to_all | solution.py:240
  40.0 109.5 %all-gather.2.cloned.1.call-start = ((), (), s32[]{:S(2)}) async-start(), calls=%async_computation.6 | async-start | bytes 4456448 | tf_op jit(solution)/shard_map/all_gather | solution.py:251
  40.8 29.4 %copy-start.8 = (f32[1,1024,128]{2,1,0:T(8,128)S(1)}, f32[1,1024,128]{2,1,0:T(8,128)}, u32[]{:S(2)}) copy-start(f32[1,1024,128]{2,1,0:T(8,128)} %param.11) | copy-start | bytes 1572868
  40.8 29.4 %copy-start.9 = (f32[1,1024,128]{2,1,0:T(8,128)S(1)}, f32[1,1024,128]{2,1,0:T(8,128)}, u32[]{:S(2)}) copy-start(f32[1,1024,128]{2,1,0:T(8,128)} %param.10) | copy-start | bytes 1572868
  59.7 20.2 %all-to-all-start.3 = ((bf16[4,5,128,128]{3,2,1,0:T(8,128)(2,1)}), bf16[4,5,128,128]{3,2,1,0:T(8,128)(2,1)S(1)}, u32[]{:S(2)}, u32[]{:S(2)}) async-start(bf16[4,5,128,128]{3,2,1,0:T(8,128)(2,1)} %get-tuple-element.22.after.refs_0_), calls=%async_computation.3 | async-start | bytes 1310720 | tf_op jit(solution)/shard_map/all_to_all | solution.py:241
  66.6 12.4 %copy-start.16 = (bf16[128,1024]{1,0:T(8,128)(2,1)S(1)}, bf16[128,1024]{1,0:T(8,128)(2,1)}, u32[]{:S(2)}) copy-start(bf16[128,1024]{1,0:T(8,128)(2,1)} %get-tuple-element.28) | copy-start | bytes 786436
  66.6 23.1 %collective-permute-start = (bf16[64,1024]{1,0:T(8,128)(2,1)}, bf16[64,1024]{1,0:T(8,128)(2,1)S(1)}, u32[]{:S(2)}, u32[]{:S(2)}) collective-permute-start(bf16[64,1024]{1,0:T(8,128)(2,1)} %get-tuple-element.24), channel_id=1, source_target_pairs={{0,64},{64,128},{128,192},{192,256},{256,320},{320,384},{384,448},... | collective-permute-start | bytes 393224 | tf_op jit(solution)/shard_map/ppermute | solution.py:266
  71.3 23.8 %collective-permute-start.3 = (bf16[64,1024]{1,0:T(8,128)(2,1)S(1)}, bf16[64,1024]{1,0:T(8,128)(2,1)S(1)}, u32[]{:S(2)}, u32[]{:S(2)}) collective-permute-start(bf16[64,1024]{1,0:T(8,128)(2,1)S(1)} %copy-done.19), channel_id=1, source_target_pairs={{0,448},{64,0},{128,64},{192,128},{256,192},{320,256},{384,320},{4... | collective-permute-start | bytes 393224 | tf_op jit(solution)/shard_map/ppermute | solution.py:267
  83.8 43.1 %all-to-all-start.4 = ((f32[16,128,128]{2,1,0:T(8,128)}), f32[16,128,128]{2,1,0:T(8,128)S(1)}, u32[]{:S(2)}, u32[]{:S(2)}) async-start(f32[16,128,128]{2,1,0:T(8,128)} %pad_maximum_fusion), calls=%async_computation.4 | async-start | bytes 2097152 | tf_op jit(solution)/shard_map/all_to_all | solution.py:261
  89.7 29.1 %copy-start.13 = (bf16[128,1024]{1,0:T(8,128)(2,1)S(1)}, bf16[128,1024]{1,0:T(8,128)(2,1)}, u32[]{:S(2)}) copy-start(bf16[128,1024]{1,0:T(8,128)(2,1)} %get-tuple-element.26) | copy-start | bytes 786436
  89.7 31.1 %copy-start.12 = (bf16[128,1024]{1,0:T(8,128)(2,1)S(1)}, bf16[128,1024]{1,0:T(8,128)(2,1)}, u32[]{:S(2)}) copy-start(bf16[128,1024]{1,0:T(8,128)(2,1)} %get-tuple-element.30) | copy-start | bytes 786436
  89.8 29.0 %collective-permute-start.1 = (bf16[128,1024]{1,0:T(8,128)(2,1)S(1)}, bf16[128,1024]{1,0:T(8,128)(2,1)S(1)}, u32[]{:S(2)}, u32[]{:S(2)}) collective-permute-start(bf16[128,1024]{1,0:T(8,128)(2,1)S(1)} %pad_maximum_fusion.1), channel_id=1, source_target_pairs={{0,64},{64,128},{128,192},{192,256},{256,320},{320,384},{384,448},... | collective-permute-start | bytes 786440 | tf_op jit(solution)/shard_map/ppermute | solution.py:266
  95.2 25.5 %collective-permute-start.4 = (bf16[128,1024]{1,0:T(8,128)(2,1)S(1)}, bf16[128,1024]{1,0:T(8,128)(2,1)S(1)}, u32[]{:S(2)}, u32[]{:S(2)}) collective-permute-start(bf16[128,1024]{1,0:T(8,128)(2,1)S(1)} %pad_maximum_fusion.2), channel_id=1, source_target_pairs={{0,448},{64,0},{128,64},{192,128},{256,192},{320,256},{384,320},{4... | collective-permute-start | bytes 786440 | tf_op jit(solution)/shard_map/ppermute | solution.py:267
  118.8 22.2 %collective-permute-start.2 = (bf16[128,1024]{1,0:T(8,128)(2,1)S(1)}, bf16[128,1024]{1,0:T(8,128)(2,1)S(1)}, u32[]{:S(2)}, u32[]{:S(2)}) collective-permute-start(bf16[128,1024]{1,0:T(8,128)(2,1)S(1)} %add_convert_fusion.3), channel_id=1, source_target_pairs={{0,64},{64,128},{128,192},{192,256},{256,320},{320,384},{384,448},... | collective-permute-start | bytes 786440 | tf_op jit(solution)/shard_map/ppermute | solution.py:266
  120.9 21.5 %collective-permute-start.5 = (bf16[128,1024]{1,0:T(8,128)(2,1)S(1)}, bf16[128,1024]{1,0:T(8,128)(2,1)S(1)}, u32[]{:S(2)}, u32[]{:S(2)}) collective-permute-start(bf16[128,1024]{1,0:T(8,128)(2,1)S(1)} %add_convert_fusion.1), channel_id=1, source_target_pairs={{0,448},{64,0},{128,64},{192,128},{256,192},{320,256},{384,320},{4... | collective-permute-start | bytes 786440 | tf_op jit(solution)/shard_map/ppermute | solution.py:267
  130.2 10.8 %copy-start.11 = (bf16[128,1024]{1,0:T(8,128)(2,1)S(1)}, bf16[128,1024]{1,0:T(8,128)(2,1)}, u32[]{:S(2)}) copy-start(bf16[128,1024]{1,0:T(8,128)(2,1)} %get-tuple-element.27) | copy-start | bytes 786436
  130.2 12.2 %copy-start.10 = (bf16[128,1024]{1,0:T(8,128)(2,1)S(1)}, bf16[128,1024]{1,0:T(8,128)(2,1)}, u32[]{:S(2)}) copy-start(bf16[128,1024]{1,0:T(8,128)(2,1)} %get-tuple-element.31) | copy-start | bytes 786436
  130.2 47.8 %all-to-all-start.5 = ((f32[16,128,128]{2,1,0:T(8,128)}), f32[16,128,128]{2,1,0:T(8,128)S(1)}, u32[]{:S(2)}, u32[]{:S(2)}) async-start(f32[16,128,128]{2,1,0:T(8,128)} %reorder.3), calls=%async_computation.5 | async-start | bytes 2097152 | tf_op jit(solution)/shard_map/all_to_all | solution.py:263
  143.2 16.4 %copy-start.3 = (bf16[128,1024]{1,0:T(8,128)(2,1)S(1)}, bf16[128,1024]{1,0:T(8,128)(2,1)}, u32[]{:S(2)}) copy-start(bf16[128,1024]{1,0:T(8,128)(2,1)} %add_convert_fusion.2.refs_0_) | copy-start | bytes 786436
  143.2 20.5 %copy-start.4 = (bf16[128,1024]{1,0:T(8,128)(2,1)S(1)}, bf16[128,1024]{1,0:T(8,128)(2,1)}, u32[]{:S(2)}) copy-start(bf16[128,1024]{1,0:T(8,128)(2,1)} %add_convert_fusion.refs_1_) | copy-start | bytes 786436
  154.6 27.5 %collective-permute-start.6 = (bf16[16,128,128]{2,1,0:T(8,128)(2,1)}, bf16[16,128,128]{2,1,0:T(8,128)(2,1)S(1)}, u32[]{:S(2)}, u32[]{:S(2)}) collective-permute-start(bf16[16,128,128]{2,1,0:T(8,128)(2,1)} %produce.3), channel_id=1, source_target_pairs={{0,16},{16,0},{1,17},{17,1},{2,18},{18,2},{3,19},{19,3},{4,20},{20... | collective-permute-start | bytes 1572872 | tf_op jit(solution)/shard_map/ppermute | solution.py:275
  159.5 13.6 %collective-permute-start.7 = (bf16[128,1024]{1,0:T(8,128)(2,1)S(1)}, bf16[128,1024]{1,0:T(8,128)(2,1)S(1)}, u32[]{:S(2)}, u32[]{:S(2)}) collective-permute-start(bf16[128,1024]{1,0:T(8,128)(2,1)S(1)} %copy-done.3), channel_id=1, source_target_pairs={{0,64},{64,128},{128,192},{192,256},{256,320},{320,384},{384,448},... | collective-permute-start | bytes 786440 | tf_op jit(solution)/shard_map/ppermute | solution.py:266
  163.7 14.2 %collective-permute-start.8 = (bf16[128,1024]{1,0:T(8,128)(2,1)S(1)}, bf16[128,1024]{1,0:T(8,128)(2,1)S(1)}, u32[]{:S(2)}, u32[]{:S(2)}) collective-permute-start(bf16[128,1024]{1,0:T(8,128)(2,1)S(1)} %copy-done.4), channel_id=1, source_target_pairs={{0,448},{64,0},{128,64},{192,128},{256,192},{320,256},{384,320},{4... | collective-permute-start | bytes 786440 | tf_op jit(solution)/shard_map/ppermute | solution.py:267
  (11 other events, 29.2 us)
Sparse Core Ops, SparseCore 0:
  42.9 106.5 all-gather.1

commit v3 on v2

--- a/solution.py
+++ b/solution.py
@@ -128,8 +128,12 @@
         member = member + 1 - 2 * lax.rem(member, 2)
     size = out.shape[1]
     mine = rows[pl.ds(pl.multiple_of(member * size, size), size), :]
-    for i in range(blocks.shape[0]):
-        out[i] = jnp.dot(mine, blocks[i], preferred_element_type=jnp.float32).astype(out.dtype)
+    columns = blocks.shape[2]
+    for i in range(0, blocks.shape[0], 2):
+        pair = jnp.concatenate([blocks[i], blocks[i + 1]], axis=1)
+        total = jnp.dot(mine, pair, preferred_element_type=jnp.float32).astype(out.dtype)
+        out[i] = total[:, :columns]
+        out[i + 1] = total[:, columns:]
 
 
 def produce(mate, place, rows, blocks, after):
@@ -275,7 +279,7 @@
     far = lax.ppermute(produce(True, place, rows, gathered, last), "half", SWAP)
     near = produce(False, place, rows, gathered, [])
     output = assemble(place, near, far)
-    new_weight, new_first, new_second = adam(moved_weight, moments, part[0], up_sum, down_sum, near)
+    new_weight, new_first, new_second = adam(moved_weight, moments, part[0], up_sum, down_sum, output)
     return (output[None], new_weight[None], new_first[None], new_second[None])
 
 

time: 193 us -> 190 us (0.984)
  the two profiles are of different devices: /device:TPU:38 before, /device:TPU:6 now
where the time goes in v3:
time: 190 us; the launch traced here: 189 us
  starting transfers between devices  69.2 us (36%)
  waiting for transfers between devices  56.2 us (30%)
  Pallas kernels  28.1 us (15%)
  between operations  14.3 us (8%)
  blocking collectives  12.1 us (6%)
  local copies, waits for them, and re-layouts  5.85 us (3%)
  other arithmetic  3.37 us (2%)
    ppermute x4, starting transfers between devices, local(): down_sum = lax.ppermute(down_sum, 'ring', DOWN)  29.5 us
    ppermute x4, waiting for transfers between devices, local(): down_sum = lax.ppermute(down_sum, 'ring', DOWN)  19.6 us
    all_to_all x1, waiting for transfers between devices, local(): one = lax.all_to_all(one, TEAM, split_axis=0, concat_axis=0, tiled=True)  19.4 us
    all_to_all x1, blocking collectives, local(): lax.all_to_all(ordered, 'expert', split_axis=0, concat_axis=0, tiled=True)  12.1 us
    pallas_call x2, Pallas kernels, produce(): pl.pallas_call(functools.partial(produce_kernel, mate), out_shape=shape((...  9.6 us
    ppermute x4, waiting for transfers between devices, local(): up_sum = lax.ppermute(up_sum, 'ring', UP)  9.3 us
    all_to_all x1, starting transfers between devices, local(): lax.all_to_all(weight.reshape(hosts, block_rows, columns), 'expert', spli...  9.22 us
    ppermute x4, starting transfers between devices, local(): up_sum = lax.ppermute(up_sum, 'ring', UP)  8.09 us
  transfers between devices with their start and end apart: 15, of which 8 were waited for; matrix products, arithmetic and copies ran while one was open for 3% of the time, Pallas kernels for 12%

profile of v3, /device:TPU:6, one launch (start us, length us, event | category | flops | bytes accessed | tf_op | source)
XLA Modules:
  0.0 189.2 jit_solution(4907225314988712515)
XLA Ops:
  7.2 9.2 %all-to-all-start.1 = ((bf16[16,64,128]{2,1,0:T(8,128)(2,1)}), bf16[16,64,128]{2,1,0:T(8,128)(2,1)S(1)}, u32[]{:S(2)}, u32[]{:S(2)}) async-start(bf16[16,64,128]{2,1,0:T(8,128)(2,1)} %bitcast.18), calls=%async_computation.1 | async-start | bytes 524288 | tf_op jit(solution)/shard_map/all_to_all | solution.py:246
  18.3 3.1 %prepare.1 = (bf16[4,11,128,128]{3,2,1,0:T(8,128)(2,1)}, bf16[4,5,128,128]{3,2,1,0:T(8,128)(2,1)}) custom-call(s32[3]{0:T(128)} %compare_select_fusion.1.place, s32[16]{0:T(128)} %new_host.5, s32[32,16]{1,0:T(8,128)} %copy.14.counts, bf16[128,1024]{1,0:T(8,128)(2,1)} %bitcast.19, bf16[128,1024]{1,0:T(8,128)(2,1)} %bitcast.20, bf16[128,4096]{1,0:T(8,128)(2,1)} %bitcast.15), custom_call_target="tpu_custom_call" | custom-call | bytes 3145728 | tf_op jit(solution)/shard_map/prepare/pallas_call | solution.py:60
  24.4 12.1 %all_to_all.30 = bf16[16,64,128]{2,1,0:T(8,128)(2,1)} all-to-all(bf16[16,64,128]{2,1,0:T(8,128)(2,1)} %reorder.2), channel_id=1, replica_groups=mesh['ring'=8,'near'=2,'half'=2,'expert'=16] {'expert'}, dimensions={0} | all-to-all | bytes 524288 | tf_op jit(solution)/shard_map/all_to_all | solution.py:250
  36.4 3.6 %all-to-all-start = ((bf16[4,11,128,128]{3,2,1,0:T(8,128)(2,1)}), bf16[4,11,128,128]{3,2,1,0:T(8,128)(2,1)S(1)}, u32[]{:S(2)}, u32[]{:S(2)}) async-start(bf16[4,11,128,128]{3,2,1,0:T(8,128)(2,1)} %get-tuple-element.21), calls=%async_computation | async-start | bytes 2883584 | tf_op jit(solution)/shard_map/all_to_all | solution.py:244
  40.7 19.4 %all-to-all-done.blocks = bf16[4,11,128,128]{3,2,1,0:T(8,128)(2,1)S(1)} async-done(((bf16[4,11,128,128]{3,2,1,0:T(8,128)(2,1)}), bf16[4,11,128,128]{3,2,1,0:T(8,128)(2,1)S(1)}, u32[]{:S(2)}, u32[]{:S(2)}) %all-to-all-start) | async-done | bytes 1441824 | tf_op jit(solution)/shard_map/all_to_all | solution.py:244
  60.2 3.5 %all-to-all-start.3 = ((bf16[4,5,128,128]{3,2,1,0:T(8,128)(2,1)}), bf16[4,5,128,128]{3,2,1,0:T(8,128)(2,1)S(1)}, u32[]{:S(2)}, u32[]{:S(2)}) async-start(bf16[4,5,128,128]{3,2,1,0:T(8,128)(2,1)} %get-tuple-element.22.after.refs_0_), calls=%async_computation.3 | async-start | bytes 1310720 | tf_op jit(solution)/shard_map/all_to_all | solution.py:245
  63.7 2.9 %first_parts.1 = (bf16[512,1024]{1,0:T(8,128)(2,1)}, bf16[64,1024]{1,0:T(8,128)(2,1)}, bf16[64,1024]{1,0:T(8,128)(2,1)}, bf16[128,1024]{1,0:T(8,128)(2,1)}, bf16[128,1024]{1,0:T(8,128)(2,1)}) custom-call(bf16[4,11,128,128]{3,2,1,0:T(8,128)(2,1)} %copy-done, bf16[4,5,128,128]{3,2,1,0:T(8,128)(2,1)} %get-tuple-element.22.after.refs_0_), custom_call_target="tpu_custom_call" | custom-call | flops 268435456 | bytes 3145728 | tf_op jit(solution)/shard_map/first_parts/pallas_call | solution.py:96
  66.5 9.4 %collective-permute-start.3 = (bf16[64,1024]{1,0:T(8,128)(2,1)}, bf16[64,1024]{1,0:T(8,128)(2,1)S(1)}, u32[]{:S(2)}, u32[]{:S(2)}) collective-permute-start(bf16[64,1024]{1,0:T(8,128)(2,1)} %get-tuple-element.29), channel_id=1, source_target_pairs={{0,448},{64,0},{128,64},{192,128},{256,192},{320,256},{384,320},{4... | collective-permute-start | bytes 393224 | tf_op jit(solution)/shard_map/ppermute | solution.py:271
  79.0 5.1 %all-to-all-done.3.blocks = bf16[4,5,128,128]{3,2,1,0:T(8,128)(2,1)S(1)} async-done(((bf16[4,5,128,128]{3,2,1,0:T(8,128)(2,1)}), bf16[4,5,128,128]{3,2,1,0:T(8,128)(2,1)S(1)}, u32[]{:S(2)}, u32[]{:S(2)}) %all-to-all-start.3) | async-done | bytes 655392 | tf_op jit(solution)/shard_map/all_to_all | solution.py:245
  85.0 3.0 %second_parts.1 = (bf16[128,1024]{1,0:T(8,128)(2,1)}, bf16[128,1024]{1,0:T(8,128)(2,1)}, bf16[128,1024]{1,0:T(8,128)(2,1)}, bf16[128,1024]{1,0:T(8,128)(2,1)}, bf16[128,1024]{1,0:T(8,128)(2,1)}) custom-call(bf16[4,5,128,128]{3,2,1,0:T(8,128)(2,1)} %copy-done.6, bf16[512,1024]{1,0:T(8,128)(2,1)} %get-tuple-element.23.rows), custom_call_target="tpu_custom_call" | custom-call | flops 536870912 | bytes 3145728 | tf_op jit(solution)/shard_map/second_parts/pallas_call | solution.py:114
  88.0 5.0 %all-to-all-start.4 = ((f32[16,128,128]{2,1,0:T(8,128)}), f32[16,128,128]{2,1,0:T(8,128)S(1)}, u32[]{:S(2)}, u32[]{:S(2)}) async-start(f32[16,128,128]{2,1,0:T(8,128)} %pad_maximum_fusion), calls=%async_computation.4 | async-start | bytes 2097152 | tf_op jit(solution)/shard_map/all_to_all | solution.py:265
  93.1 9.2 %collective-permute-start.4 = (bf16[128,1024]{1,0:T(8,128)(2,1)S(1)}, bf16[128,1024]{1,0:T(8,128)(2,1)S(1)}, u32[]{:S(2)}, u32[]{:S(2)}) collective-permute-start(bf16[128,1024]{1,0:T(8,128)(2,1)S(1)} %pad_maximum_fusion.2), channel_id=1, source_target_pairs={{0,448},{64,0},{128,64},{192,128},{256,192},{320,256},{384,320},{4... | collective-permute-start | bytes 786440 | tf_op jit(solution)/shard_map/ppermute | solution.py:271
  104.3 15.1 %collective-permute-done.4 = bf16[128,1024]{1,0:T(8,128)(2,1)S(1)} collective-permute-done((bf16[128,1024]{1,0:T(8,128)(2,1)S(1)}, bf16[128,1024]{1,0:T(8,128)(2,1)S(1)}, u32[]{:S(2)}, u32[]{:S(2)}) %collective-permute-start.4) | collective-permute-done | bytes 262176 | tf_op jit(solution)/shard_map/ppermute | solution.py:271
  119.4 6.5 %collective-permute-start.5 = (bf16[128,1024]{1,0:T(8,128)(2,1)S(1)}, bf16[128,1024]{1,0:T(8,128)(2,1)S(1)}, u32[]{:S(2)}, u32[]{:S(2)}) collective-permute-start(bf16[128,1024]{1,0:T(8,128)(2,1)S(1)} %add_convert_fusion.1), channel_id=1, source_target_pairs={{0,448},{64,0},{128,64},{192,128},{256,192},{320,256},{384,320},{4... | collective-permute-start | bytes 786440 | tf_op jit(solution)/shard_map/ppermute | solution.py:271
  131.3 5.6 %all-to-all-start.5 = ((f32[16,128,128]{2,1,0:T(8,128)}), f32[16,128,128]{2,1,0:T(8,128)S(1)}, u32[]{:S(2)}, u32[]{:S(2)}) async-start(f32[16,128,128]{2,1,0:T(8,128)} %reorder.3), calls=%async_computation.5 | async-start | bytes 2097152 | tf_op jit(solution)/shard_map/all_to_all | solution.py:267
  136.8 4.5 %collective-permute-done.5 = bf16[128,1024]{1,0:T(8,128)(2,1)S(1)} collective-permute-done((bf16[128,1024]{1,0:T(8,128)(2,1)S(1)}, bf16[128,1024]{1,0:T(8,128)(2,1)S(1)}, u32[]{:S(2)}, u32[]{:S(2)}) %collective-permute-start.5) | collective-permute-done | bytes 262176 | tf_op jit(solution)/shard_map/ppermute | solution.py:271
  142.1 6.0 %collective-permute-done.2 = bf16[128,1024]{1,0:T(8,128)(2,1)S(1)} collective-permute-done((bf16[128,1024]{1,0:T(8,128)(2,1)S(1)}, bf16[128,1024]{1,0:T(8,128)(2,1)S(1)}, u32[]{:S(2)}, u32[]{:S(2)}) %collective-permute-start.2) | collective-permute-done | bytes 262176 | tf_op jit(solution)/shard_map/ppermute | solution.py:270
  150.3 4.8 %produce.3 = bf16[16,128,128]{2,1,0:T(8,128)(2,1)} custom-call(s32[3]{0:T(128)} %compare_select_fusion.1.place, bf16[512,1024]{1,0:T(8,128)(2,1)} %get-tuple-element.23.rows, bf16[16,1024,128]{2,1,0:T(8,128)(2,1)} %all-gather.2.cloned.1.call-done.blocks, bf16[128,1024]{1,0:T(8,128)(2,1)} %add_convert_fusion.2.refs_0_, bf16[128,1024]{1,0:T(8,128)(2,1)} %add_convert_fusion.refs_1_), custom_call_target="tpu_custom_call" | custom-call | flops 536870912 | bytes 5242880 | tf_op jit(solution)/shard_map/produce/pallas_call | solution.py:142
  155.1 4.9 %collective-permute-start.6 = (bf16[16,128,128]{2,1,0:T(8,128)(2,1)}, bf16[16,128,128]{2,1,0:T(8,128)(2,1)S(1)}, u32[]{:S(2)}, u32[]{:S(2)}) collective-permute-start(bf16[16,128,128]{2,1,0:T(8,128)(2,1)} %produce.3), channel_id=1, source_target_pairs={{0,16},{16,0},{1,17},{17,1},{2,18},{18,2},{3,19},{19,3},{4,20},{20... | collective-permute-start | bytes 1572872 | tf_op jit(solution)/shard_map/ppermute | solution.py:279
  160.0 4.4 %collective-permute-start.8 = (bf16[128,1024]{1,0:T(8,128)(2,1)S(1)}, bf16[128,1024]{1,0:T(8,128)(2,1)S(1)}, u32[]{:S(2)}, u32[]{:S(2)}) collective-permute-start(bf16[128,1024]{1,0:T(8,128)(2,1)S(1)} %copy-done.3), channel_id=1, source_target_pairs={{0,448},{64,0},{128,64},{192,128},{256,192},{320,256},{384,320},{4... | collective-permute-start | bytes 786440 | tf_op jit(solution)/shard_map/ppermute | solution.py:271
  166.8 4.8 %produce.2.near = bf16[16,128,128]{2,1,0:T(8,128)(2,1)} custom-call(s32[3]{0:T(128)} %compare_select_fusion.1.place, bf16[512,1024]{1,0:T(8,128)(2,1)} %get-tuple-element.23.rows, bf16[16,1024,128]{2,1,0:T(8,128)(2,1)} %all-gather.2.cloned.1.call-done.blocks), custom_call_target="tpu_custom_call" | custom-call | flops 536870912 | bytes 5242880 | tf_op jit(solution)/shard_map/produce/pallas_call | solution.py:142
  172.4 2.5 %assemble.1.after = bf16[128,4096]{1,0:T(8,128)(2,1)} custom-call(s32[3]{0:T(128)} %compare_select_fusion.1.place, bf16[16,128,128]{2,1,0:T(8,128)(2,1)} %produce.2.near, bf16[16,128,128]{2,1,0:T(8,128)(2,1)} %copy-done.7), custom_call_target="tpu_custom_call" | custom-call | bytes 2097152 | tf_op jit(solution)/shard_map/assemble/pallas_call | solution.py:184
  174.8 3.3 %collective-permute-done.7.rising = bf16[128,1024]{1,0:T(8,128)(2,1)S(1)} collective-permute-done((bf16[128,1024]{1,0:T(8,128)(2,1)S(1)}, bf16[128,1024]{1,0:T(8,128)(2,1)S(1)}, u32[]{:S(2)}, u32[]{:S(2)}) %collective-permute-start.7) | collective-permute-done | bytes 262176 | tf_op jit(solution)/shard_map/ppermute | solution.py:270
  179.3 3.0 %adam.1 = (bf16[1024,128]{1,0:T(8,128)(2,1)}, f32[1024,128]{1,0:T(8,128)}, f32[1024,128]{1,0:T(8,128)}) custom-call(bf16[1024,128]{1,0:T(8,128)(2,1)} %bitcast.14, f32[16,128,128]{2,1,0:T(8,128)} %copy-done.1, bf16[128,1024]{1,0:T(8,128)(2,1)} %get-tuple-element.34.part, bf16[128,1024]{1,0:T(8,128)(2,1)} %copy-done.15, bf16[128,1024]{1,0:T(8,128)(2,1)} %copy-done.14, ...), custom_call_target="tpu_custom_call" | custom-call | bytes 3145728 | tf_op jit(solution)/shard_map/adam/pallas_call | solution.py:213
  (70 shorter events, 24.1 us)
Async XLA Ops:
  7.2 14.8 %all-to-all-start.1 = ((bf16[16,64,128]{2,1,0:T(8,128)(2,1)}), bf16[16,64,128]{2,1,0:T(8,128)(2,1)S(1)}, u32[]{:S(2)}, u32[]{:S(2)}) async-start(bf16[16,64,128]{2,1,0:T(8,128)(2,1)} %bitcast.18), calls=%async_computation.1 | async-start | bytes 524288 | tf_op jit(solution)/shard_map/all_to_all | solution.py:246
  36.4 23.7 %all-to-all-start = ((bf16[4,11,128,128]{3,2,1,0:T(8,128)(2,1)}), bf16[4,11,128,128]{3,2,1,0:T(8,128)(2,1)S(1)}, u32[]{:S(2)}, u32[]{:S(2)}) async-start(bf16[4,11,128,128]{3,2,1,0:T(8,128)(2,1)} %get-tuple-element.21), calls=%async_computation | async-start | bytes 2883584 | tf_op jit(solution)/shard_map/all_to_all | solution.py:244
  40.0 110.4 %all-gather.2.cloned.1.call-start = ((), (), s32[]{:S(2)}) async-start(), calls=%async_computation.6 | async-start | bytes 4456448 | tf_op jit(solution)/shard_map/all_gather | solution.py:255
  40.7 35.2 %copy-start.8 = (f32[1,1024,128]{2,1,0:T(8,128)S(1)}, f32[1,1024,128]{2,1,0:T(8,128)}, u32[]{:S(2)}) copy-start(f32[1,1024,128]{2,1,0:T(8,128)} %param.11) | copy-start | bytes 1572868
  40.7 35.2 %copy-start.9 = (f32[1,1024,128]{2,1,0:T(8,128)S(1)}, f32[1,1024,128]{2,1,0:T(8,128)}, u32[]{:S(2)}) copy-start(f32[1,1024,128]{2,1,0:T(8,128)} %param.10) | copy-start | bytes 1572868
  60.2 24.0 %all-to-all-start.3 = ((bf16[4,5,128,128]{3,2,1,0:T(8,128)(2,1)}), bf16[4,5,128,128]{3,2,1,0:T(8,128)(2,1)S(1)}, u32[]{:S(2)}, u32[]{:S(2)}) async-start(bf16[4,5,128,128]{3,2,1,0:T(8,128)(2,1)} %get-tuple-element.22.after.refs_0_), calls=%async_computation.3 | async-start | bytes 1310720 | tf_op jit(solution)/shard_map/all_to_all | solution.py:245
  66.5 10.5 %copy-start.19 = (bf16[64,1024]{1,0:T(8,128)(2,1)S(1)}, bf16[64,1024]{1,0:T(8,128)(2,1)}, u32[]{:S(2)}) copy-start(bf16[64,1024]{1,0:T(8,128)(2,1)} %get-tuple-element.24) | copy-start | bytes 393220
  66.5 12.4 %copy-start.16 = (bf16[128,1024]{1,0:T(8,128)(2,1)S(1)}, bf16[128,1024]{1,0:T(8,128)(2,1)}, u32[]{:S(2)}) copy-start(bf16[128,1024]{1,0:T(8,128)(2,1)} %get-tuple-element.25) | copy-start | bytes 786436
  66.5 26.4 %collective-permute-start.3 = (bf16[64,1024]{1,0:T(8,128)(2,1)}, bf16[64,1024]{1,0:T(8,128)(2,1)S(1)}, u32[]{:S(2)}, u32[]{:S(2)}) collective-permute-start(bf16[64,1024]{1,0:T(8,128)(2,1)} %get-tuple-element.29), channel_id=1, source_target_pairs={{0,448},{64,0},{128,64},{192,128},{256,192},{320,256},{384,320},{4... | collective-permute-start | bytes 393224 | tf_op jit(solution)/shard_map/ppermute | solution.py:271
  77.0 25.2 %collective-permute-start = (bf16[64,1024]{1,0:T(8,128)(2,1)S(1)}, bf16[64,1024]{1,0:T(8,128)(2,1)S(1)}, u32[]{:S(2)}, u32[]{:S(2)}) collective-permute-start(bf16[64,1024]{1,0:T(8,128)(2,1)S(1)} %copy-done.19), channel_id=1, source_target_pairs={{0,64},{64,128},{128,192},{192,256},{256,320},{320,384},{384,448},... | collective-permute-start | bytes 393224 | tf_op jit(solution)/shard_map/ppermute | solution.py:270
  88.0 40.0 %all-to-all-start.4 = ((f32[16,128,128]{2,1,0:T(8,128)}), f32[16,128,128]{2,1,0:T(8,128)S(1)}, u32[]{:S(2)}, u32[]{:S(2)}) async-start(f32[16,128,128]{2,1,0:T(8,128)} %pad_maximum_fusion), calls=%async_computation.4 | async-start | bytes 2097152 | tf_op jit(solution)/shard_map/all_to_all | solution.py:265
  93.0 26.4 %copy-start.13 = (bf16[128,1024]{1,0:T(8,128)(2,1)S(1)}, bf16[128,1024]{1,0:T(8,128)(2,1)}, u32[]{:S(2)}) copy-start(bf16[128,1024]{1,0:T(8,128)(2,1)} %get-tuple-element.30) | copy-start | bytes 786436
  93.0 33.0 %copy-start.12 = (bf16[128,1024]{1,0:T(8,128)(2,1)S(1)}, bf16[128,1024]{1,0:T(8,128)(2,1)}, u32[]{:S(2)}) copy-start(bf16[128,1024]{1,0:T(8,128)(2,1)} %get-tuple-element.26) | copy-start | bytes 786436
  93.1 26.3 %collective-permute-start.4 = (bf16[128,1024]{1,0:T(8,128)(2,1)S(1)}, bf16[128,1024]{1,0:T(8,128)(2,1)S(1)}, u32[]{:S(2)}, u32[]{:S(2)}) collective-permute-start(bf16[128,1024]{1,0:T(8,128)(2,1)S(1)} %pad_maximum_fusion.2), channel_id=1, source_target_pairs={{0,448},{64,0},{128,64},{192,128},{256,192},{320,256},{384,320},{4... | collective-permute-start | bytes 786440 | tf_op jit(solution)/shard_map/ppermute | solution.py:271
  102.4 23.6 %collective-permute-start.1 = (bf16[128,1024]{1,0:T(8,128)(2,1)S(1)}, bf16[128,1024]{1,0:T(8,128)(2,1)S(1)}, u32[]{:S(2)}, u32[]{:S(2)}) collective-permute-start(bf16[128,1024]{1,0:T(8,128)(2,1)S(1)} %pad_maximum_fusion.1), channel_id=1, source_target_pairs={{0,64},{64,128},{128,192},{192,256},{256,320},{320,384},{384,448},... | collective-permute-start | bytes 786440 | tf_op jit(solution)/shard_map/ppermute | solution.py:270
  119.4 21.9 %collective-permute-start.5 = (bf16[128,1024]{1,0:T(8,128)(2,1)S(1)}, bf16[128,1024]{1,0:T(8,128)(2,1)S(1)}, u32[]{:S(2)}, u32[]{:S(2)}) collective-permute-start(bf16[128,1024]{1,0:T(8,128)(2,1)S(1)} %add_convert_fusion.1), channel_id=1, source_target_pairs={{0,448},{64,0},{128,64},{192,128},{256,192},{320,256},{384,320},{4... | collective-permute-start | bytes 786440 | tf_op jit(solution)/shard_map/ppermute | solution.py:271
  126.0 22.0 %collective-permute-start.2 = (bf16[128,1024]{1,0:T(8,128)(2,1)S(1)}, bf16[128,1024]{1,0:T(8,128)(2,1)S(1)}, u32[]{:S(2)}, u32[]{:S(2)}) collective-permute-start(bf16[128,1024]{1,0:T(8,128)(2,1)S(1)} %add_convert_fusion.3), channel_id=1, source_target_pairs={{0,64},{64,128},{128,192},{192,256},{256,320},{320,384},{384,448},... | collective-permute-start | bytes 786440 | tf_op jit(solution)/shard_map/ppermute | solution.py:270
  131.3 16.8 %copy-start.10 = (bf16[128,1024]{1,0:T(8,128)(2,1)S(1)}, bf16[128,1024]{1,0:T(8,128)(2,1)}, u32[]{:S(2)}) copy-start(bf16[128,1024]{1,0:T(8,128)(2,1)} %get-tuple-element.27) | copy-start | bytes 786436
  131.3 46.9 %all-to-all-start.5 = ((f32[16,128,128]{2,1,0:T(8,128)}), f32[16,128,128]{2,1,0:T(8,128)S(1)}, u32[]{:S(2)}, u32[]{:S(2)}) async-start(f32[16,128,128]{2,1,0:T(8,128)} %reorder.3), calls=%async_computation.5 | async-start | bytes 2097152 | tf_op jit(solution)/shard_map/all_to_all | solution.py:267
  148.8 11.2 %copy-start.3 = (bf16[128,1024]{1,0:T(8,128)(2,1)S(1)}, bf16[128,1024]{1,0:T(8,128)(2,1)}, u32[]{:S(2)}) copy-start(bf16[128,1024]{1,0:T(8,128)(2,1)} %add_convert_fusion.refs_1_) | copy-start | bytes 786436
  148.8 15.6 %copy-start.4 = (bf16[128,1024]{1,0:T(8,128)(2,1)S(1)}, bf16[128,1024]{1,0:T(8,128)(2,1)}, u32[]{:S(2)}) copy-start(bf16[128,1024]{1,0:T(8,128)(2,1)} %add_convert_fusion.2.refs_0_) | copy-start | bytes 786436
  155.1 16.5 %collective-permute-start.6 = (bf16[16,128,128]{2,1,0:T(8,128)(2,1)}, bf16[16,128,128]{2,1,0:T(8,128)(2,1)S(1)}, u32[]{:S(2)}, u32[]{:S(2)}) collective-permute-start(bf16[16,128,128]{2,1,0:T(8,128)(2,1)} %produce.3), channel_id=1, source_target_pairs={{0,16},{16,0},{1,17},{17,1},{2,18},{18,2},{3,19},{19,3},{4,20},{20... | collective-permute-start | bytes 1572872 | tf_op jit(solution)/shard_map/ppermute | solution.py:279
  160.0 14.8 %collective-permute-start.8 = (bf16[128,1024]{1,0:T(8,128)(2,1)S(1)}, bf16[128,1024]{1,0:T(8,128)(2,1)S(1)}, u32[]{:S(2)}, u32[]{:S(2)}) collective-permute-start(bf16[128,1024]{1,0:T(8,128)(2,1)S(1)} %copy-done.3), channel_id=1, source_target_pairs={{0,448},{64,0},{128,64},{192,128},{256,192},{320,256},{384,320},{4... | collective-permute-start | bytes 786440 | tf_op jit(solution)/shard_map/ppermute | solution.py:271
  164.4 13.7 %collective-permute-start.7 = (bf16[128,1024]{1,0:T(8,128)(2,1)S(1)}, bf16[128,1024]{1,0:T(8,128)(2,1)S(1)}, u32[]{:S(2)}, u32[]{:S(2)}) collective-permute-start(bf16[128,1024]{1,0:T(8,128)(2,1)S(1)} %copy-done.4), channel_id=1, source_target_pairs={{0,64},{64,128},{128,192},{192,256},{256,320},{320,384},{384,448},... | collective-permute-start | bytes 786440 | tf_op jit(solution)/shard_map/ppermute | solution.py:270
  (11 other events, 37.5 us)
Sparse Core Ops, SparseCore 0:
  42.9 107.4 all-gather.1

commit v4 on v3

--- a/solution.py
+++ b/solution.py
@@ -105,20 +105,20 @@
     )(blocks, after)
 
 
-def second_kernel(blocks, rows, *out):
+def second_kernel(blocks, rows, after, *out):
     for i, ref in enumerate(out):
         ref[...] = part_of(blocks, i, rows)
 
 
-def second_parts(blocks, rows):
+def second_parts(blocks, rows, after):
     return pl.pallas_call(
         second_kernel,
         out_shape=[shape((blocks.shape[3], rows.shape[1]))] * len(SECOND),
-        in_specs=[VMEM] * 2,
+        in_specs=[VMEM] * 2 + [ANY],
         out_specs=[VMEM] * len(SECOND),
         cost_estimate=cost(1 << 29, 3 << 20),
         name="second_parts",
-    )(blocks, rows)
+    )(blocks, rows, after)
 
 
 def produce_kernel(mate, place, rows, blocks, *refs):
@@ -199,8 +199,8 @@
     for d in range(hosts):
         at = pl.ds(d * step, step)
         g = grad[d * step : (d + 1) * step]
-        first = beta_one * moments[d, :step] + (1.0 - beta_one) * g
-        second = beta_two * moments[d, step:] + (1.0 - beta_two) * g * g
+        first = beta_one * moments[d, :step].astype(jnp.float32) + (1.0 - beta_one) * g
+        second = beta_two * moments[d, step:].astype(jnp.float32) + (1.0 - beta_two) * g * g
         update = (
             learning_rate * (first / bias_one) / (jnp.sqrt(second / bias_two) + epsilon_value)
         )
@@ -241,34 +241,38 @@
 
     one, two = prepare(place, new_host, counts, gate_act[0], up_act[0], out_grad[0])
     order = two
-    one = lax.all_to_all(one, TEAM, split_axis=0, concat_axis=0, tiled=True)
-    two = lax.all_to_all(two, TEAM, split_axis=0, concat_axis=0, tiled=True)
     spread = lax.all_to_all(
         weight.reshape(hosts, block_rows, columns), "expert", split_axis=0, concat_axis=0, tiled=True
     )
     ordered = reorder(spread, old_host, new_host, [order])
     moved_weight = lax.all_to_all(ordered, "expert", split_axis=0, concat_axis=0, tiled=True)
     moved_weight = moved_weight.reshape(hidden_units, columns)
+    one, moved_weight = lax.optimization_barrier((one, moved_weight))
+    one = lax.all_to_all(one, TEAM, split_axis=0, concat_axis=0, tiled=True)
+    two = lax.all_to_all(two, TEAM, split_axis=0, concat_axis=0, tiled=True)
     rows, low, high, *part = first_parts(one, order)
-    part = dict(zip(FIRST[1:] + SECOND, [*part, *second_parts(two, rows)]))
+    part = dict(zip(FIRST[1:], part))
 
     gathered = lax.all_gather(moved_weight, ("ring", "near"), axis=0, tiled=False)
     up_sum, down_sum = low, high
-    stacked = jnp.concatenate(
-        [
-            first_moment.reshape(hosts, block_rows, columns),
-            second_moment.reshape(hosts, block_rows, columns),
-        ],
-        axis=1,
-    )
-    stacked, part[0] = lax.optimization_barrier((stacked, part[0]))
-    spread = lax.all_to_all(stacked, "expert", split_axis=0, concat_axis=0, tiled=True)
-    ordered = reorder(spread, old_host, new_host, [])
-    moments = lax.all_to_all(ordered, "expert", split_axis=0, concat_axis=0, tiled=True)
     for step in range(1, N_FAR // 2 + 1):
-        last = [up_sum, down_sum]
+        if step == 3:
+            last = [up_sum, down_sum]
         up_sum = lax.ppermute(up_sum, "ring", UP)
         down_sum = lax.ppermute(down_sum, "ring", DOWN)
+        if step == 1:
+            part |= zip(SECOND, second_parts(two, rows, up_sum))
+            stacked = jnp.concatenate(
+                [
+                    first_moment.reshape(hosts, block_rows, columns),
+                    second_moment.reshape(hosts, block_rows, columns),
+                ],
+                axis=1,
+            ).astype(jnp.bfloat16)
+            stacked, part[0] = lax.optimization_barrier((stacked, part[0]))
+            spread = lax.all_to_all(stacked, "expert", split_axis=0, concat_axis=0, tiled=True)
+            ordered = reorder(spread, old_host, new_host, [])
+            moments = lax.all_to_all(ordered, "expert", split_axis=0, concat_axis=0, tiled=True)
         if step < N_FAR // 2:
             up_part, down_part = part[N_FAR // 2 - step], part[step - N_FAR // 2]
             if step == 1:

time: 190 us -> 184 us (0.968)
  waiting for transfers between devices: 56.2 us -> 25.2 us
  blocking collectives: 12.1 us -> 38.5 us
    all_to_all x0 -> x1, blocking collectives: none -> 26.4 us  [local(): one = lax.all_to_all(one, TEAM, split_axis=0, concat_axis=0, tiled=True)]
    all_to_all x1 -> x0, waiting for transfers between devices: 19.4 us -> none  [local(): one = lax.all_to_all(one, TEAM, split_axis=0, concat_axis=0, tiled=True)]
    ppermute x4, waiting for transfers between devices: 19.6 us -> 4.72 us  [local(): down_sum = lax.ppermute(down_sum, 'ring', DOWN)]
    all_gather x1, waiting for transfers between devices: 1.5 us -> 13.7 us  [local(): lax.all_gather(moved_weight, ('ring', 'near'), axis=0, tiled=False)]
    all_to_all x1, waiting for transfers between devices: 5.15 us -> 0.01 us  [local(): two = lax.all_to_all(two, TEAM, split_axis=0, concat_axis=0, tiled=True)]
    all_to_all x1 -> x0, starting transfers between devices: 3.55 us -> none  [local(): one = lax.all_to_all(one, TEAM, split_axis=0, concat_axis=0, tiled=True)]
    ppermute x4, waiting for transfers between devices: 9.3 us -> 6.28 us  [local(): up_sum = lax.ppermute(up_sum, 'ring', UP)]
    unnamed x41 -> x39, local copies, waits for them, and re-layouts: 5.83 us -> 6.03 us
  transfers between devices with their start and end apart: 15 -> 14, of which waited for: 8 -> 5; matrix products, arithmetic and copies ran while one was open for 3% -> 2% of each run, Pallas kernels for 12% -> 13%
where the time goes in v4:
time: 184 us; the launch traced here: 182 us
  starting transfers between devices  67.4 us (37%)
  blocking collectives  38.5 us (21%)
  Pallas kernels  27.8 us (15%)
  waiting for transfers between devices  25.2 us (14%)
  between operations  14.4 us (8%)
  local copies, waits for them, and re-layouts  6.05 us (3%)
  other arithmetic  2.77 us (2%)
    ppermute x4, starting transfers between devices, local(): down_sum = lax.ppermute(down_sum, 'ring', DOWN)  29.2 us
    all_to_all x1, blocking collectives, local(): one = lax.all_to_all(one, TEAM, split_axis=0, concat_axis=0, tiled=True)  26.4 us
    all_gather x1, waiting for transfers between devices, local(): lax.all_gather(moved_weight, ('ring', 'near'), axis=0, tiled=False)  13.7 us
    all_to_all x1, blocking collectives, local(): lax.all_to_all(ordered, 'expert', split_axis=0, concat_axis=0, tiled=True)  12.1 us
    pallas_call x2, Pallas kernels, produce(): pl.pallas_call(functools.partial(produce_kernel, mate), out_shape=shape((...  9.67 us
    ppermute x4, starting transfers between devices, local(): up_sum = lax.ppermute(up_sum, 'ring', UP)  9.55 us
    all_to_all x1, starting transfers between devices, local(): lax.all_to_all(weight.reshape(hosts, block_rows, columns), 'expert', spli...  9.22 us
    ppermute x4, waiting for transfers between devices, local(): up_sum = lax.ppermute(up_sum, 'ring', UP)  6.28 us
  transfers between devices with their start and end apart: 14, of which 5 were waited for; matrix products, arithmetic and copies ran while one was open for 2% of the time, Pallas kernels for 13%

profile of v4, /device:TPU:6, one launch (start us, length us, event | category | flops | bytes accessed | tf_op | source)
XLA Modules:
  0.0 182.0 jit_solution(4520351413133067134)
XLA Ops:
  7.2 9.2 %all-to-all-start = ((bf16[16,64,128]{2,1,0:T(8,128)(2,1)}), bf16[16,64,128]{2,1,0:T(8,128)(2,1)S(1)}, u32[]{:S(2)}, u32[]{:S(2)}) async-start(bf16[16,64,128]{2,1,0:T(8,128)(2,1)} %bitcast.20), calls=%async_computation | async-start | bytes 524288 | tf_op jit(solution)/shard_map/all_to_all | solution.py:244
  18.4 3.2 %prepare.1 = (bf16[4,11,128,128]{3,2,1,0:T(8,128)(2,1)}, bf16[4,5,128,128]{3,2,1,0:T(8,128)(2,1)}) custom-call(s32[3]{0:T(128)} %compare_select_fusion.1.place, s32[16]{0:T(128)} %new_host.5, s32[32,16]{1,0:T(8,128)} %copy.13.counts, bf16[128,1024]{1,0:T(8,128)(2,1)} %bitcast.21, bf16[128,1024]{1,0:T(8,128)(2,1)} %bitcast.22, bf16[128,4096]{1,0:T(8,128)(2,1)} %bitcast.17), custom_call_target="tpu_custom_call" | custom-call | bytes 3145728 | tf_op jit(solution)/shard_map/prepare/pallas_call | solution.py:60
  24.4 12.1 %all_to_all.30 = bf16[16,64,128]{2,1,0:T(8,128)(2,1)} all-to-all(bf16[16,64,128]{2,1,0:T(8,128)(2,1)} %reorder.2), channel_id=1, replica_groups=mesh['ring'=8,'near'=2,'half'=2,'expert'=16] {'expert'}, dimensions={0} | all-to-all | bytes 524288 | tf_op jit(solution)/shard_map/all_to_all | solution.py:248
  36.5 26.4 %all_to_all.31.blocks = bf16[4,11,128,128]{3,2,1,0:T(8,128)(2,1)} all-to-all(bf16[4,11,128,128]{3,2,1,0:T(8,128)(2,1)S(1)} %copy-done.2), channel_id=1, replica_groups=mesh['ring'=8,'near'=2,'half'=2,'expert'=16] {'near','half'}, dimensions={0} | all-to-all | bytes 2883584 | tf_op jit(solution)/shard_map/all_to_all | solution.py:251
  62.9 3.6 %all-to-all-start.3 = ((bf16[4,5,128,128]{3,2,1,0:T(8,128)(2,1)}), bf16[4,5,128,128]{3,2,1,0:T(8,128)(2,1)S(1)}, u32[]{:S(2)}, u32[]{:S(2)}) async-start(bf16[4,5,128,128]{3,2,1,0:T(8,128)(2,1)} %get-tuple-element.24.refs_0_.after), calls=%async_computation.3 | async-start | bytes 1310720 | tf_op jit(solution)/shard_map/all_to_all | solution.py:252
  66.5 2.9 %first_parts.1 = (bf16[512,1024]{1,0:T(8,128)(2,1)}, bf16[64,1024]{1,0:T(8,128)(2,1)}, bf16[64,1024]{1,0:T(8,128)(2,1)}, bf16[128,1024]{1,0:T(8,128)(2,1)}, bf16[128,1024]{1,0:T(8,128)(2,1)}) custom-call(bf16[4,11,128,128]{3,2,1,0:T(8,128)(2,1)} %all_to_all.31.blocks, bf16[4,5,128,128]{3,2,1,0:T(8,128)(2,1)} %get-tuple-element.24.refs_0_.after), custom_call_target="tpu_custom_call" | custom-call | flops 268435456 | bytes 3145728 | tf_op jit(solution)/shard_map/first_parts/pallas_call | solution.py:96
  69.5 13.5 %collective-permute-start.2 = (bf16[64,1024]{1,0:T(8,128)(2,1)}, bf16[64,1024]{1,0:T(8,128)(2,1)S(1)}, u32[]{:S(2)}, u32[]{:S(2)}) collective-permute-start(bf16[64,1024]{1,0:T(8,128)(2,1)} %get-tuple-element.32), channel_id=1, source_target_pairs={{0,448},{64,0},{128,64},{192,128},{256,192},{320,256},{384,320},{4... | collective-permute-start | bytes 393224 | tf_op jit(solution)/shard_map/ppermute | solution.py:262
  83.9 1.9 %collective-permute-start = (bf16[64,1024]{1,0:T(8,128)(2,1)S(1)}, bf16[64,1024]{1,0:T(8,128)(2,1)S(1)}, u32[]{:S(2)}, u32[]{:S(2)}) collective-permute-start(bf16[64,1024]{1,0:T(8,128)(2,1)S(1)} %copy-done.18), channel_id=1, source_target_pairs={{0,64},{64,128},{128,192},{192,256},{256,320},{320,384},{384,448},... | collective-permute-start | bytes 393224 | tf_op jit(solution)/shard_map/ppermute | solution.py:261
  85.9 4.7 %collective-permute-done.2 = bf16[64,1024]{1,0:T(8,128)(2,1)S(1)} collective-permute-done((bf16[64,1024]{1,0:T(8,128)(2,1)}, bf16[64,1024]{1,0:T(8,128)(2,1)S(1)}, u32[]{:S(2)}, u32[]{:S(2)}) %collective-permute-start.2) | collective-permute-done | bytes 131104 | tf_op jit(solution)/shard_map/ppermute | solution.py:262
  90.6 6.7 %collective-permute-start.3 = (bf16[128,1024]{1,0:T(8,128)(2,1)S(1)}, bf16[128,1024]{1,0:T(8,128)(2,1)S(1)}, u32[]{:S(2)}, u32[]{:S(2)}) collective-permute-start(bf16[128,1024]{1,0:T(8,128)(2,1)S(1)} %pad_maximum_fusion.2), channel_id=1, source_target_pairs={{0,448},{64,0},{128,64},{192,128},{256,192},{320,256},{384,320},{4... | collective-permute-start | bytes 786440 | tf_op jit(solution)/shard_map/ppermute | solution.py:262
  97.4 3.6 %collective-permute-done.after = bf16[64,1024]{1,0:T(8,128)(2,1)S(1)} collective-permute-done((bf16[64,1024]{1,0:T(8,128)(2,1)S(1)}, bf16[64,1024]{1,0:T(8,128)(2,1)S(1)}, u32[]{:S(2)}, u32[]{:S(2)}) %collective-permute-start) | collective-permute-done | bytes 131104 | tf_op jit(solution)/shard_map/ppermute | solution.py:261
  103.8 3.1 %second_parts.1 = (bf16[128,1024]{1,0:T(8,128)(2,1)}, bf16[128,1024]{1,0:T(8,128)(2,1)}, bf16[128,1024]{1,0:T(8,128)(2,1)}, bf16[128,1024]{1,0:T(8,128)(2,1)}, bf16[128,1024]{1,0:T(8,128)(2,1)}) custom-call(bf16[4,5,128,128]{3,2,1,0:T(8,128)(2,1)} %copy-done.6, bf16[512,1024]{1,0:T(8,128)(2,1)} %get-tuple-element.26.rows, bf16[64,1024]{1,0:T(8,128)(2,1)} %copy-done.17), custom_call_target="tpu_custom_call" | custom-call | flops 536870912 | bytes 3145728 | tf_op jit(solution)/shard_map/second_parts/pallas_call | solution.py:114
  106.9 5.4 %all-to-all-start.4 = ((bf16[16,128,128]{2,1,0:T(8,128)(2,1)}), bf16[16,128,128]{2,1,0:T(8,128)(2,1)S(1)}, u32[]{:S(2)}, u32[]{:S(2)}) async-start(bf16[16,128,128]{2,1,0:T(8,128)(2,1)} %pad_maximum_fusion), calls=%async_computation.4 | async-start | bytes 1048576 | tf_op jit(solution)/shard_map/all_to_all | solution.py:273
  113.3 6.0 %collective-permute-start.7 = (bf16[128,1024]{1,0:T(8,128)(2,1)S(1)}, bf16[128,1024]{1,0:T(8,128)(2,1)S(1)}, u32[]{:S(2)}, u32[]{:S(2)}) collective-permute-start(bf16[128,1024]{1,0:T(8,128)(2,1)S(1)} %add_convert_fusion.2.refs_1_), channel_id=1, source_target_pairs={{0,448},{64,0},{128,64},{192,128},{256,192},{320,256},{384,320},{4... | collective-permute-start | bytes 786440 | tf_op jit(solution)/shard_map/ppermute | solution.py:262
  124.1 5.8 %all-to-all-start.5 = ((bf16[16,128,128]{2,1,0:T(8,128)(2,1)}), bf16[16,128,128]{2,1,0:T(8,128)(2,1)S(1)}, u32[]{:S(2)}, u32[]{:S(2)}) async-start(bf16[16,128,128]{2,1,0:T(8,128)(2,1)} %reorder.3), calls=%async_computation.5 | async-start | bytes 1048576 | tf_op jit(solution)/shard_map/all_to_all | solution.py:275
  129.8 13.7 %all-gather.3.cloned.1.call-done = bf16[16384,128]{1,0:T(8,128)(2,1)} async-done(((bf16[1024,128]{1,0:T(8,128)(2,1)}), bf16[16384,128]{1,0:T(8,128)(2,1)}) %all-gather.3.cloned.1.call-update) | async-done | bytes 4194320 | tf_op jit(solution)/shard_map/all_gather | solution.py:256
  143.5 4.9 %produce.3 = bf16[16,128,128]{2,1,0:T(8,128)(2,1)} custom-call(s32[3]{0:T(128)} %compare_select_fusion.1.place, bf16[512,1024]{1,0:T(8,128)(2,1)} %get-tuple-element.26.rows, bf16[16,1024,128]{2,1,0:T(8,128)(2,1)} %bitcast.12, bf16[128,1024]{1,0:T(8,128)(2,1)} %copy-done.4, bf16[128,1024]{1,0:T(8,128)(2,1)} %copy-done.3), custom_call_target="tpu_custom_call" | custom-call | flops 536870912 | bytes 5242880 | tf_op jit(solution)/shard_map/produce/pallas_call | solution.py:142
  148.4 4.7 %collective-permute-start.4 = (bf16[16,128,128]{2,1,0:T(8,128)(2,1)}, bf16[16,128,128]{2,1,0:T(8,128)(2,1)S(1)}, u32[]{:S(2)}, u32[]{:S(2)}) collective-permute-start(bf16[16,128,128]{2,1,0:T(8,128)(2,1)} %produce.3), channel_id=1, source_target_pairs={{0,16},{16,0},{1,17},{17,1},{2,18},{18,2},{3,19},{19,3},{4,20},{20... | collective-permute-start | bytes 1572872 | tf_op jit(solution)/shard_map/ppermute | solution.py:283
  153.2 3.0 %collective-permute-start.8 = (bf16[128,1024]{1,0:T(8,128)(2,1)S(1)}, bf16[128,1024]{1,0:T(8,128)(2,1)S(1)}, u32[]{:S(2)}, u32[]{:S(2)}) collective-permute-start(bf16[128,1024]{1,0:T(8,128)(2,1)S(1)} %add_convert_fusion), channel_id=1, source_target_pairs={{0,448},{64,0},{128,64},{192,128},{256,192},{320,256},{384,320},{4... | collective-permute-start | bytes 786440 | tf_op jit(solution)/shard_map/ppermute | solution.py:262
  156.3 3.8 %collective-permute-start.6 = (bf16[128,1024]{1,0:T(8,128)(2,1)S(1)}, bf16[128,1024]{1,0:T(8,128)(2,1)S(1)}, u32[]{:S(2)}, u32[]{:S(2)}) collective-permute-start(bf16[128,1024]{1,0:T(8,128)(2,1)S(1)} %add_convert_fusion.1), channel_id=1, source_target_pairs={{0,64},{64,128},{128,192},{192,256},{256,320},{320,384},{384,448},... | collective-permute-start | bytes 786440 | tf_op jit(solution)/shard_map/ppermute | solution.py:261
  160.1 4.8 %produce.2.near = bf16[16,128,128]{2,1,0:T(8,128)(2,1)} custom-call(s32[3]{0:T(128)} %compare_select_fusion.1.place, bf16[512,1024]{1,0:T(8,128)(2,1)} %get-tuple-element.26.rows, bf16[16,1024,128]{2,1,0:T(8,128)(2,1)} %bitcast.13), custom_call_target="tpu_custom_call" | custom-call | flops 536870912 | bytes 5242880 | tf_op jit(solution)/shard_map/produce/pallas_call | solution.py:142
  165.7 2.5 %assemble.1.after = bf16[128,4096]{1,0:T(8,128)(2,1)} custom-call(s32[3]{0:T(128)} %compare_select_fusion.1.place, bf16[16,128,128]{2,1,0:T(8,128)(2,1)} %produce.2.near, bf16[16,128,128]{2,1,0:T(8,128)(2,1)} %copy-done.7), custom_call_target="tpu_custom_call" | custom-call | bytes 2097152 | tf_op jit(solution)/shard_map/assemble/pallas_call | solution.py:184
  168.1 2.7 %collective-permute-done.6.rising = bf16[128,1024]{1,0:T(8,128)(2,1)S(1)} collective-permute-done((bf16[128,1024]{1,0:T(8,128)(2,1)S(1)}, bf16[128,1024]{1,0:T(8,128)(2,1)S(1)}, u32[]{:S(2)}, u32[]{:S(2)}) %collective-permute-start.6) | collective-permute-done | bytes 262176 | tf_op jit(solution)/shard_map/ppermute | solution.py:261
  172.3 2.9 %adam.1 = (bf16[1024,128]{1,0:T(8,128)(2,1)}, f32[1024,128]{1,0:T(8,128)}, f32[1024,128]{1,0:T(8,128)}) custom-call(bf16[1024,128]{1,0:T(8,128)(2,1)} %bitcast.16, bf16[16,128,128]{2,1,0:T(8,128)(2,1)} %copy-done, bf16[128,1024]{1,0:T(8,128)(2,1)} %get-tuple-element.36.part, bf16[128,1024]{1,0:T(8,128)(2,1)} %copy-done.13, bf16[128,1024]{1,0:T(8,128)(2,1)} %copy-done.12, ...), custom_call_target="tpu_custom_call" | custom-call | bytes 3145728 | tf_op jit(solution)/shard_map/adam/pallas_call | solution.py:213
  (69 shorter events, 16.7 us)
Async XLA Ops:
  7.2 14.8 %all-to-all-start = ((bf16[16,64,128]{2,1,0:T(8,128)(2,1)}), bf16[16,64,128]{2,1,0:T(8,128)(2,1)S(1)}, u32[]{:S(2)}, u32[]{:S(2)}) async-start(bf16[16,64,128]{2,1,0:T(8,128)(2,1)} %bitcast.20), calls=%async_computation | async-start | bytes 524288 | tf_op jit(solution)/shard_map/all_to_all | solution.py:244
  16.4 127.2 %all-gather.3.cloned.1.call-start = ((), (), s32[]{:S(2)}) async-start(), calls=%async_computation.6 | async-start | bytes 4456448 | tf_op jit(solution)/shard_map/all_gather | solution.py:256
  21.5 14.9 %copy-start.2 = (bf16[4,11,128,128]{3,2,1,0:T(8,128)(2,1)S(1)}, bf16[4,11,128,128]{3,2,1,0:T(8,128)(2,1)}, u32[]{:S(2)}) copy-start(bf16[4,11,128,128]{3,2,1,0:T(8,128)(2,1)} %get-tuple-element.25) | copy-start | bytes 4325380
  62.9 20.1 %copy-start.8 = (f32[1,1024,128]{2,1,0:T(8,128)S(1)}, f32[1,1024,128]{2,1,0:T(8,128)}, u32[]{:S(2)}) copy-start(f32[1,1024,128]{2,1,0:T(8,128)} %param.10) | copy-start | bytes 1572868
  62.9 40.1 %all-to-all-start.3 = ((bf16[4,5,128,128]{3,2,1,0:T(8,128)(2,1)}), bf16[4,5,128,128]{3,2,1,0:T(8,128)(2,1)S(1)}, u32[]{:S(2)}, u32[]{:S(2)}) async-start(bf16[4,5,128,128]{3,2,1,0:T(8,128)(2,1)} %get-tuple-element.24.refs_0_.after), calls=%async_computation.3 | async-start | bytes 1310720 | tf_op jit(solution)/shard_map/all_to_all | solution.py:252
  66.5 16.5 %copy-start.9 = (f32[1,1024,128]{2,1,0:T(8,128)S(1)}, f32[1,1024,128]{2,1,0:T(8,128)}, u32[]{:S(2)}) copy-start(f32[1,1024,128]{2,1,0:T(8,128)} %param.11) | copy-start | bytes 1572868
  69.5 14.4 %copy-start.16 = (bf16[128,1024]{1,0:T(8,128)(2,1)S(1)}, bf16[128,1024]{1,0:T(8,128)(2,1)}, u32[]{:S(2)}) copy-start(bf16[128,1024]{1,0:T(8,128)(2,1)} %get-tuple-element.31) | copy-start | bytes 786436
  69.5 14.4 %copy-start.18 = (bf16[64,1024]{1,0:T(8,128)(2,1)S(1)}, bf16[64,1024]{1,0:T(8,128)(2,1)}, u32[]{:S(2)}) copy-start(bf16[64,1024]{1,0:T(8,128)(2,1)} %get-tuple-element.28) | copy-start | bytes 393220
  69.5 16.4 %copy-start.15 = (bf16[128,1024]{1,0:T(8,128)(2,1)S(1)}, bf16[128,1024]{1,0:T(8,128)(2,1)}, u32[]{:S(2)}) copy-start(bf16[128,1024]{1,0:T(8,128)(2,1)} %get-tuple-element.29) | copy-start | bytes 786436
  69.5 21.1 %collective-permute-start.2 = (bf16[64,1024]{1,0:T(8,128)(2,1)}, bf16[64,1024]{1,0:T(8,128)(2,1)S(1)}, u32[]{:S(2)}, u32[]{:S(2)}) collective-permute-start(bf16[64,1024]{1,0:T(8,128)(2,1)} %get-tuple-element.32), channel_id=1, source_target_pairs={{0,448},{64,0},{128,64},{192,128},{256,192},{320,256},{384,320},{4... | collective-permute-start | bytes 393224 | tf_op jit(solution)/shard_map/ppermute | solution.py:262
  83.9 17.0 %collective-permute-start = (bf16[64,1024]{1,0:T(8,128)(2,1)S(1)}, bf16[64,1024]{1,0:T(8,128)(2,1)S(1)}, u32[]{:S(2)}, u32[]{:S(2)}) collective-permute-start(bf16[64,1024]{1,0:T(8,128)(2,1)S(1)} %copy-done.18), channel_id=1, source_target_pairs={{0,64},{64,128},{128,192},{192,256},{256,320},{320,384},{384,448},... | collective-permute-start | bytes 393224 | tf_op jit(solution)/shard_map/ppermute | solution.py:261
  90.6 21.6 %collective-permute-start.3 = (bf16[128,1024]{1,0:T(8,128)(2,1)S(1)}, bf16[128,1024]{1,0:T(8,128)(2,1)S(1)}, u32[]{:S(2)}, u32[]{:S(2)}) collective-permute-start(bf16[128,1024]{1,0:T(8,128)(2,1)S(1)} %pad_maximum_fusion.2), channel_id=1, source_target_pairs={{0,448},{64,0},{128,64},{192,128},{256,192},{320,256},{384,320},{4... | collective-permute-start | bytes 786440 | tf_op jit(solution)/shard_map/ppermute | solution.py:262
  101.0 18.3 %collective-permute-start.1 = (bf16[128,1024]{1,0:T(8,128)(2,1)S(1)}, bf16[128,1024]{1,0:T(8,128)(2,1)S(1)}, u32[]{:S(2)}, u32[]{:S(2)}) collective-permute-start(bf16[128,1024]{1,0:T(8,128)(2,1)S(1)} %pad_maximum_fusion.1), channel_id=1, source_target_pairs={{0,64},{64,128},{128,192},{192,256},{256,320},{320,384},{384,448},... | collective-permute-start | bytes 786440 | tf_op jit(solution)/shard_map/ppermute | solution.py:261
  106.9 12.5 %copy-start.14 = (bf16[128,1024]{1,0:T(8,128)(2,1)S(1)}, bf16[128,1024]{1,0:T(8,128)(2,1)}, u32[]{:S(2)}) copy-start(bf16[128,1024]{1,0:T(8,128)(2,1)} %get-tuple-element.30) | copy-start | bytes 786436
  106.9 14.5 %all-to-all-start.4 = ((bf16[16,128,128]{2,1,0:T(8,128)(2,1)}), bf16[16,128,128]{2,1,0:T(8,128)(2,1)S(1)}, u32[]{:S(2)}, u32[]{:S(2)}) async-start(bf16[16,128,128]{2,1,0:T(8,128)(2,1)} %pad_maximum_fusion), calls=%async_computation.4 | async-start | bytes 1048576 | tf_op jit(solution)/shard_map/all_to_all | solution.py:273
  113.3 10.8 %copy-start.3 = (bf16[128,1024]{1,0:T(8,128)(2,1)}, bf16[128,1024]{1,0:T(8,128)(2,1)S(1)}, u32[]{:S(2)}) copy-start(bf16[128,1024]{1,0:T(8,128)(2,1)S(1)} %add_convert_fusion.2.refs_1_) | copy-start | bytes 786436
  113.3 39.8 %collective-permute-start.7 = (bf16[128,1024]{1,0:T(8,128)(2,1)S(1)}, bf16[128,1024]{1,0:T(8,128)(2,1)S(1)}, u32[]{:S(2)}, u32[]{:S(2)}) collective-permute-start(bf16[128,1024]{1,0:T(8,128)(2,1)S(1)} %add_convert_fusion.2.refs_1_), channel_id=1, source_target_pairs={{0,448},{64,0},{128,64},{192,128},{256,192},{320,256},{384,320},{4... | collective-permute-start | bytes 786440 | tf_op jit(solution)/shard_map/ppermute | solution.py:262
  119.4 24.1 %copy-start.4 = (bf16[128,1024]{1,0:T(8,128)(2,1)}, bf16[128,1024]{1,0:T(8,128)(2,1)S(1)}, u32[]{:S(2)}) copy-start(bf16[128,1024]{1,0:T(8,128)(2,1)S(1)} %add_convert_fusion.3.refs_0_) | copy-start | bytes 786436
  119.4 36.7 %collective-permute-start.5 = (bf16[128,1024]{1,0:T(8,128)(2,1)S(1)}, bf16[128,1024]{1,0:T(8,128)(2,1)S(1)}, u32[]{:S(2)}, u32[]{:S(2)}) collective-permute-start(bf16[128,1024]{1,0:T(8,128)(2,1)S(1)} %add_convert_fusion.3.refs_0_), channel_id=1, source_target_pairs={{0,64},{64,128},{128,192},{192,256},{256,320},{320,384},{384,448},... | collective-permute-start | bytes 786440 | tf_op jit(solution)/shard_map/ppermute | solution.py:261
  124.1 46.8 %all-to-all-start.5 = ((bf16[16,128,128]{2,1,0:T(8,128)(2,1)}), bf16[16,128,128]{2,1,0:T(8,128)(2,1)S(1)}, u32[]{:S(2)}, u32[]{:S(2)}) async-start(bf16[16,128,128]{2,1,0:T(8,128)(2,1)} %reorder.3), calls=%async_computation.5 | async-start | bytes 1048576 | tf_op jit(solution)/shard_map/all_to_all | solution.py:275
  143.5 12.6 %copy-start.10 = (bf16[128,1024]{1,0:T(8,128)(2,1)S(1)}, bf16[128,1024]{1,0:T(8,128)(2,1)}, u32[]{:S(2)}) copy-start(bf16[128,1024]{1,0:T(8,128)(2,1)} %get-tuple-element.37) | copy-start | bytes 786436
  148.4 16.5 %collective-permute-start.4 = (bf16[16,128,128]{2,1,0:T(8,128)(2,1)}, bf16[16,128,128]{2,1,0:T(8,128)(2,1)S(1)}, u32[]{:S(2)}, u32[]{:S(2)}) collective-permute-start(bf16[16,128,128]{2,1,0:T(8,128)(2,1)} %produce.3), channel_id=1, source_target_pairs={{0,16},{16,0},{1,17},{17,1},{2,18},{18,2},{3,19},{19,3},{4,20},{20... | collective-permute-start | bytes 1572872 | tf_op jit(solution)/shard_map/ppermute | solution.py:283
  153.2 14.9 %collective-permute-start.8 = (bf16[128,1024]{1,0:T(8,128)(2,1)S(1)}, bf16[128,1024]{1,0:T(8,128)(2,1)S(1)}, u32[]{:S(2)}, u32[]{:S(2)}) collective-permute-start(bf16[128,1024]{1,0:T(8,128)(2,1)S(1)} %add_convert_fusion), channel_id=1, source_target_pairs={{0,448},{64,0},{128,64},{192,128},{256,192},{320,256},{384,320},{4... | collective-permute-start | bytes 786440 | tf_op jit(solution)/shard_map/ppermute | solution.py:262
  156.3 14.6 %collective-permute-start.6 = (bf16[128,1024]{1,0:T(8,128)(2,1)S(1)}, bf16[128,1024]{1,0:T(8,128)(2,1)S(1)}, u32[]{:S(2)}, u32[]{:S(2)}) collective-permute-start(bf16[128,1024]{1,0:T(8,128)(2,1)S(1)} %add_convert_fusion.1), channel_id=1, source_target_pairs={{0,64},{64,128},{128,192},{192,256},{256,320},{320,384},{384,448},... | collective-permute-start | bytes 786440 | tf_op jit(solution)/shard_map/ppermute | solution.py:261
  (9 other events, 18.9 us)
Sparse Core Ops, SparseCore 0:
  36.6 106.9 all-gather.2
